TPU v7x, 32 devices: a whole 2x2x4 slice. The times are simulated.
32 devices in a mesh: shard: 8 (over z, x), replica: 4 (over y, core).
Axes of the slice: x: 2, y: 2, z: 4, core: 2. Of those that a mesh axis runs over, the one named last changes fastest.
Arguments:
- momentum: bfloat16 [1, 4, 4096, 4096], P(None, 'replica', 'shard'), may hold values from -36 to 36
- grad: bfloat16 [1, 4, 4096, 4096], P(None, 'replica', 'shard'), may hold values from -6 to 6
- right_prev: bfloat16 [1, 4096, 256], P(None, 'shard'), may hold values from -6 to 6
Outputs:
- momentum_new: bfloat16 [1, 4, 4096, 4096], P(None, 'replica', 'shard')
- update: bfloat16 [1, 4096, 4096], P(None, 'shard')
- right_factor: bfloat16 [1, 4096, 256], P(None, 'shard')
All inputs are finite; a program needn't handle non-finite values.
Results may differ from a plain program's by a relative error of at most 0.0095.
Values may be sent and summed in bfloat16 or wider, within the bound.
A program may use at most 64 MiB of HBM per device.

v0:
```python
import math

import jax
import jax.numpy as jnp
from jax import lax
from jax.sharding import PartitionSpec as P

momentum_decay = 0.95
epsilon_norm = 1e-06


def orthonormal(gram, block):
    chol = jnp.linalg.cholesky(gram)
    return lax.linalg.triangular_solve(chol, block, left_side=False, lower=True, transpose_a=True)


def shards(momentum, grad, right_prev):
    rows = grad.shape[2]
    width = grad.shape[3]
    rank = right_prev.shape[2]
    replicas = lax.axis_size("replica")
    factor = width / math.sqrt(rank)
    buffer = momentum[0, 0].astype(jnp.float32) + grad[0, 0].astype(jnp.float32)
    buffer_b = buffer.astype(jnp.bfloat16)

    def add_columns(total, piece, start, source=buffer_b):
        return jnp.dot(source, piece, preferred_element_type=jnp.float32)

    local_left = add_columns(
        jnp.zeros((rows, rank), jnp.float32),
        lax.all_gather(right_prev[0], "shard", axis=0, tiled=True),
        jnp.int32(0),
    )
    summed = lax.psum(local_left, "replica")
    gram = lax.psum(jnp.dot(summed.T, summed, precision=lax.Precision.HIGHEST), "shard")
    ortho = orthonormal(gram, summed)
    ortho_b = ortho.astype(jnp.bfloat16)

    def project(start, count, source=buffer_b, factor_rows=ortho_b):
        return lax.dot_general(
            source, factor_rows, (((0,), (0,)), ((), ())), preferred_element_type=jnp.float32
        )

    block_sum = lax.psum_scatter(
        project(jnp.int32(0), rows * lax.axis_size("shard")),
        "shard",
        scatter_dimension=0,
        tiled=True,
    )
    right_part = lax.psum(block_sum, "replica") / replicas
    squares = lax.psum(jnp.sum(right_part * right_part, axis=0), "shard")
    right_own = right_part.astype(jnp.bfloat16)
    right_full = lax.all_gather(right_own, "shard", axis=0, tiled=True)
    norms = jnp.sqrt(squares + epsilon_norm)
    scaled = (ortho * (factor / norms)).astype(jnp.bfloat16)
    feedback = lax.dot_general(
        ortho_b, right_full, (((1,), (1,)), ((), ())), preferred_element_type=jnp.float32
    )
    momenta = [(buffer - (1.0 - momentum_decay) * feedback).astype(jnp.bfloat16)]
    stepped = lax.dot_general(
        scaled, right_full, (((1,), (1,)), ((), ())), preferred_element_type=jnp.float32
    )
    updates = [stepped.astype(jnp.bfloat16)]
    rights = [right_own]
    return (jnp.stack(momenta)[:, None], jnp.stack(updates), jnp.stack(rights))


def solution(mesh):
    return jax.shard_map(
        shards,
        mesh=mesh,
        in_specs=(
            P(None, "replica", "shard", None),
            P(None, "replica", "shard", None),
            P(None, "shard", None),
        ),
        out_specs=(
            P(None, "replica", "shard", None),
            P(None, "shard", None),
            P(None, "shard", None),
        ),
        check_vma=False,
    )
```

profile of v0, /device:TPU:0, one launch (start us, length us, event | category | flops | bytes accessed | tf_op | source)
XLA Modules:
  0.0 439.6 jit_solution(4316823155859081388)
XLA Ops:
  7.2 0.7 all-gather.6.cloned.1.call-update
  7.9 54.0 %all-gather.6.cloned.1.call-done = bf16[1,4096,256]{2,1,0:T(8,128)(2,1)} async-done(((bf16[1,512,256]{2,1,0:T(8,128)(2,1)}), bf16[1,4096,256]{2,1,0:T(8,128)(2,1)}) %all-gather.6.cloned.1.call-update) | async-done | bytes 2097168 | tf_op jit(solution)/shard_map/all_gather | solution.py:31
  62.0 6.1 %fusion.3 = f32[512,256]{1,0:T(8,128)} fusion(bf16[1,4096,256]{2,1,0:T(8,128)(2,1)} %all-gather.6.cloned.1.call-done, bf16[1,1,512,4096]{3,2,1,0:T(8,128)(2,1)} %param.4, bf16[1,1,512,4096]{3,2,1,0:T(8,128)(2,1)} %param.3), kind=kOutput, calls=%fused_computation.9 | convolution fusion | flops 1082130432 | bytes 11010048 | tf_op jit(solution)/shard_map/dot_general | solution.py:27
  68.1 32.0 %all-reduce.5.cloned.1.call-done = f32[512,256]{1,0:T(8,128)} async-done(((f32[512,256]{1,0:T(8,128)}), f32[512,256]{1,0:T(8,128)}) %all-reduce.5.cloned.1.call-update) | async-done | bytes 524304 | tf_op jit(solution)/shard_map/psum | solution.py:34
  100.2 3.0 fusion.22
  103.2 0.2 reduce-scatter.2.cloned.1.call-start
  103.4 71.9 %all-reduce.7.cloned.1.call-done = f32[256,256]{0,1:T(8,128)} async-done(((f32[256,256]{0,1:T(8,128)}), f32[256,256]{0,1:T(8,128)}) %all-reduce.7.cloned.1.call-update) | async-done | bytes 262160 | tf_op jit(solution)/shard_map/psum | solution.py:35
  175.3 1.1 copy.7
  176.4 1.0 fusion.9
  177.4 11.7 %cholesky.50 = f32[128,128]{1,0:T(8,128)S(1)} custom-call(f32[128,128]{1,0:T(8,128)S(1)} %cholesky.118), custom_call_target="Cholesky" | custom-call | tf_op jit(solution)/shard_map/jit(cholesky)/cholesky | solution.py:13
  189.1 9.8 %custom-call.14 = f32[1,128,128]{1,2,0:T(8,128)S(1)} custom-call(f32[1,128,128]{2,1,0:T(8,128)S(1)} %get-tuple-element.26), custom_call_target="InvertDiagBlocksLowerTriangular" | custom-call | tf_op jit(solution)/shard_map/jit(cholesky)/cholesky | solution.py:13
  199.0 0.2 constant_dynamic-update-slice_fusion.1
  199.2 0.3 convolution_subtract_fusion.1
  199.4 11.7 %cholesky.105 = f32[128,128]{1,0:T(8,128)S(1)} custom-call(f32[128,128]{1,0:T(8,128)S(1)} %convolution_subtract_fusion.1), custom_call_target="Cholesky" | custom-call | tf_op jit(solution)/shard_map/jit(cholesky)/cholesky | solution.py:13
  211.2 0.6 compare_reduce_fusion
  213.2 4.2 while.1
  213.4 0.6 fusion.32
  214.0 1.4 bitcast_dynamic-update-slice_fusion.2
  215.4 0.6 fusion.32
  216.0 1.4 bitcast_dynamic-update-slice_fusion.2
  217.4 19.7 %custom-call.15 = f32[2,128,128]{1,2,0:T(8,128)S(1)} custom-call(f32[2,128,128]{2,1,0:T(8,128)S(1)} %get-tuple-element.10), custom_call_target="InvertDiagBlocksLowerTriangular" | custom-call | tf_op jit(solution)/shard_map/triangular_solve | solution.py:14
  237.1 0.4 fusion.7
  237.5 0.6 convolution_subtract_fusion
  238.1 0.4 fusion.11
  238.6 7.5 %fusion.5 = f32[4096,256]{1,0:T(8,128)} fusion(bf16[1,1,512,4096]{3,2,1,0:T(8,128)(2,1)} %param.4, bf16[1,1,512,4096]{3,2,1,0:T(8,128)(2,1)} %param.3, f32[512,128]{0,1:T(8,128)S(1)} %fusion.11, f32[512,128]{0,1:T(8,128)S(1)} %fusion.7), kind=kOutput, calls=%fused_computation.11 | convolution fusion | flops 1082654720 | bytes 13107200 | tf_op jit(solution)/shard_map/dot_general | solution.py:40
  246.2 88.0 %reduce-scatter.2.cloned.1.call-done = f32[512,256]{1,0:T(8,128)} async-done(((f32[4096,256]{1,0:T(8,128)}), f32[512,256]{1,0:T(8,128)}) %reduce-scatter.2.cloned.1.call-update) | async-done | bytes 524304 | tf_op jit(solution)/shard_map/reduce_scatter | solution.py:44
  334.2 35.2 %all-reduce.9.cloned.1.call-done = f32[512,256]{1,0:T(8,128)} async-done(((f32[512,256]{1,0:T(8,128)}), f32[512,256]{1,0:T(8,128)}) %all-reduce.9.cloned.1.call-update) | async-done | bytes 524304 | tf_op jit(solution)/shard_map/psum | solution.py:50
  369.4 1.8 multiply_reduce_fusion
  371.3 21.5 %psum.31 = f32[256]{0:T(256)S(1)} all-reduce(f32[256]{0:T(256)S(1)} %get-tuple-element.21), channel_id=1, replica_groups=mesh['shard'=8,'replica'=4] {'shard'}, use_global_device_ids=true, to_apply=%region_9.10 | all-reduce | flops 256 | bytes 2048 | tf_op jit(solution)/shard_map/psum | solution.py:51
  392.8 28.5 %all-gather.4.cloned.1.call-done = bf16[4096,256]{1,0:T(8,128)(2,1)} async-done(((bf16[512,256]{1,0:T(8,128)(2,1)}), bf16[4096,256]{1,0:T(8,128)(2,1)}) %all-gather.4.cloned.1.call-update) | async-done | bytes 2097168 | tf_op jit(solution)/shard_map/all_gather | solution.py:53
  421.3 8.0 %fusion.2 = bf16[1,1,512,4096]{3,2,1,0:T(8,128)(2,1)} fusion(bf16[4096,256]{1,0:T(8,128)(2,1)} %all-gather.4.cloned.1.call-done, bf16[1,1,512,4096]{3,2,1,0:T(8,128)(2,1)} %param.4, bf16[1,1,512,4096]{3,2,1,0:T(8,128)(2,1)} %param.3, f32[512,128]{0,1:T(8,128)S(1)} %fusion.11, f32[512,128]{0,1:T(8,128)S(1)} %fusion.7), kind=kOutput, calls=%fused_computation.8 | convolution fusion | flops 1086849024 | bytes 15204352 | tf_op jit(solution)/shard_map/dot_general | solution.py:56
  429.3 3.4 fusion.1
  (25 shorter events, 0.5 us)
Async XLA Ops:
  7.2 54.8 %all-gather.6.cloned.1.call-start = ((), (), s32[]{:S(2)}) async-start(), calls=%async_computation.6 | async-start | bytes 2359296 | tf_op jit(solution)/shard_map/all_gather | solution.py:31
  7.9 92.3 %all-reduce.5.cloned.1.call-start = ((), (), s32[]{:S(2)}) async-start(), calls=%async_computation.1 | async-start | bytes 1048576 | tf_op jit(solution)/shard_map/psum | solution.py:34
  68.1 107.2 %all-reduce.7.cloned.1.call-start = ((), (), s32[]{:S(2)}) async-start(), calls=%async_computation.2 | async-start | bytes 524288 | tf_op jit(solution)/shard_map/psum | solution.py:35
  100.2 136.9 %copy-start.1 = (f32[512,256]{1,0:T(8,128)S(1)}, f32[512,256]{1,0:T(8,128)}, u32[]{:S(2)}) copy-start(f32[512,256]{1,0:T(8,128)} %all-reduce.5.cloned.1.call-done) | copy-start | bytes 1572868
  103.2 231.0 %reduce-scatter.2.cloned.1.call-start = ((), (), s32[]{:S(2)}) async-start(), calls=%async_computation.3 | async-start | bytes 4718592 | tf_op jit(solution)/shard_map/reduce_scatter | solution.py:44
  246.1 123.3 %all-reduce.9.cloned.1.call-start = ((), (), s32[]{:S(2)}) async-start(), calls=%async_computation.4 | async-start | bytes 1048576 | tf_op jit(solution)/shard_map/psum | solution.py:50
  334.2 87.1 %all-gather.4.cloned.1.call-start = ((), (), s32[]{:S(2)}) async-start(), calls=%async_computation.5 | async-start | bytes 2359296 | tf_op jit(solution)/shard_map/all_gather | solution.py:53
  421.3 8.0 %copy-start = (bf16[4096,256]{1,0:T(8,128)(2,1)S(1)}, bf16[4096,256]{1,0:T(8,128)(2,1)}, u32[]{:S(2)}) copy-start(bf16[4096,256]{1,0:T(8,128)(2,1)} %all-gather.4.cloned.1.call-done) | copy-start | bytes 6291460
Sparse Core Ops, SparseCore 0:
  10.1 51.8 all-gather.5
  68.2 31.9 all-reduce.4
  104.1 71.1 all-reduce.6
  246.2 87.8 reduce-scatter.1
  336.3 33.0 all-reduce.8
  372.0 49.2 all-gather.3
where the time goes:
time: 440 us
  waiting for transfers between devices  310 us (70%)
  other arithmetic  56.5 us (13%)
  matrix products  29.9 us (7%)
  blocking collectives  21.5 us (5%)
  between operations  15.5 us (4%)
  local copies, waits for them, and re-layouts  5.13 us (1%)
    reduce_scatter x1, waiting for transfers between devices, shards(): lax.psum_scatter(project(jnp.int32(0), rows * lax.axis_size('shard')), 's...  88 us
    psum x1, waiting for transfers between devices, shards(): lax.psum(jnp.dot(summed.T, summed, precision=lax.Precision.HIGHEST), 'sha...  71.9 us
    all_gather x1, waiting for transfers between devices, shards(): lax.all_gather(right_prev[0], 'shard', axis=0, tiled=True)  54 us
    psum x1, waiting for transfers between devices, shards(): right_part = lax.psum(block_sum, 'replica') / replicas  35.2 us
    another operation x6, other arithmetic, orthonormal(): chol = jnp.linalg.cholesky(gram)  34 us
    psum x1, waiting for transfers between devices, shards(): summed = lax.psum(local_left, 'replica')  32 us
    all_gather x1, waiting for transfers between devices, shards(): right_full = lax.all_gather(right_own, 'shard', axis=0, tiled=True)  28.5 us
    psum x1, blocking collectives, shards(): squares = lax.psum(jnp.sum(right_part * right_part, axis=0), 'shard')  21.5 us
  transfers between devices with their start and end apart: 6, of which 6 were waited for; matrix products, arithmetic and copies ran while one was open for 0% of the time, Pallas kernels for 0%

commit v1 on v0

v1 whole, which is shorter than its diff:
```python
import functools
import math

import jax
import jax.numpy as jnp
from jax import lax
from jax.experimental import pallas as pl
from jax.experimental.pallas import tpu as pltpu
from jax.sharding import PartitionSpec as P

momentum_decay = 0.95
epsilon_norm = 1e-06
MESH = pl.DeviceIdType.MESH
HIGHEST = lax.Precision.HIGHEST
F32 = jnp.float32
BF16 = jnp.bfloat16
BLOCK = 32
MAX_COPIES = 96


def grid_of(shards_n, replicas_n):
    x = math.isqrt(shards_n // 2)
    if x < 1 or 2 * x * x != shards_n:
        x = 1
    c = 2 if replicas_n % 2 == 0 else 1
    return shards_n // x, x, replicas_n // c, c


class Net:
    def __init__(self, dims, send, recv):
        self.dims = dims
        _, nx, _, nc = dims
        s = lax.axis_index("shard")
        r = lax.axis_index("replica")
        self.at = [s // nx, s % nx, r // nc, r % nc]
        self.send, self.recv, self.used = send, recv, 0

    def device(self, axis, coordinate):
        place = list(self.at)
        place[axis] = coordinate
        return {
            "shard": place[0] * self.dims[1] + place[1],
            "replica": place[2] * self.dims[3] + place[3],
        }

    def peers(self, axis):
        n, me = self.dims[axis], self.at[axis]
        return [((me + d) % n, (me + n - d) % n) for d in range(1, n)]

    def barrier(self):
        sem = pltpu.get_barrier_semaphore()
        count = 0
        for axis in range(4):
            for target, _ in self.peers(axis):
                pl.semaphore_signal(sem, inc=1, device_id=self.device(axis, target), device_id_type=MESH)
                count += 1
        pl.semaphore_wait(sem, count)

    def start(self, src, dst, axis, target):
        i = self.used
        self.used += 1
        copy = pltpu.make_async_remote_copy(
            src_ref=src,
            dst_ref=dst,
            send_sem=self.send.at[i],
            recv_sem=self.recv.at[i],
            device_id=self.device(axis, target),
            device_id_type=MESH,
        )
        copy.start()
        return copy


def gather_all(net, own, out):
    z, x, y, c = net.at
    half = out.shape[-1] // 2
    a, b = pl.ds(0, half), pl.ds(half, half)
    others = net.peers(3)
    sent = []

    def forward(view):
        for oc, _ in others:
            sent.append(net.start(view, view, 3, oc))

    first = [(net.start(own, out.at[z, x, y, c], 0, t), f) for t, f in net.peers(0)]
    for oc, _ in others:
        sent.append(net.start(own, out.at[z, x, y, c], 3, oc))
    for copy, f in first:
        copy.wait()
    for copy, f in first:
        forward(out.at[f, x, y, c])
    mine_a, mine_b = out.at[:, x, y, c, :, a], out.at[:, x, y, c, :, b]
    second = [(net.start(mine_a, mine_a, 1, t), out.at[:, f, y, c, :, a]) for t, f in net.peers(1)]
    second += [(net.start(mine_b, mine_b, 2, t), out.at[:, x, f, c, :, b]) for t, f in net.peers(2)]
    for copy, _ in second:
        copy.wait()
    mine_a, mine_b = out.at[:, :, y, c, :, a], out.at[:, x, :, c, :, b]
    third = [(net.start(mine_a, mine_a, 2, t), out.at[:, :, f, c, :, a]) for t, f in net.peers(2)]
    third += [(net.start(mine_b, mine_b, 1, t), out.at[:, f, :, c, :, b]) for t, f in net.peers(1)]
    for _, view in second:
        forward(view)
    for copy, _ in third:
        copy.wait()
    for _, view in third:
        forward(view)
    for copy in sent:
        copy.wait()


def gather_kernel(dims, block, out, send, recv, local):
    net = Net(dims, send, recv)
    z, x, y, c = net.at
    own = pltpu.make_async_copy(block.at[y, c], out.at[z, x, y, c], local)
    own.start()
    net.barrier()
    own.wait()
    gather_all(net, block.at[y, c], out)


def left_kernel(dims, part, left, gram, rc, acc, ry, g, rgc, g1, rgy, g2, rgx, g3, gz, send, recv):
    net = Net(dims, send, recv)
    z, x, y, c = net.at
    net.barrier()
    copies = [net.start(part.at[:, t], rc.at[d], 3, t) for d, (t, _) in enumerate(net.peers(3))]
    for copy in copies:
        copy.wait()
    total = part[:, c]
    for d in range(len(copies)):
        total = total + rc[d]
    acc[...] = total
    copies = [net.start(acc.at[t], ry.at[d], 2, t) for d, (t, _) in enumerate(net.peers(2))]
    for copy in copies:
        copy.wait()
    own = acc[y]
    for d in range(len(copies)):
        own = own + ry[d]
    left[y, c] = own
    rows = [net.start(left.at[y, c], left.at[y, c], 2, t) for t, _ in net.peers(2)]
    product = lax.dot_general(own, own, (((0,), (0,)), ((), ())), precision=HIGHEST, preferred_element_type=F32)
    g[...] = product.reshape(g.shape)
    copies = [net.start(g.at[t], rgc.at[d], 3, t) for d, (t, _) in enumerate(net.peers(3))]
    for copy in copies:
        copy.wait()
    total = g[c]
    for d in range(len(copies)):
        total = total + rgc[d]
    g1[...] = total
    copies = [net.start(g1.at[t], rgy.at[d], 2, t) for d, (t, _) in enumerate(net.peers(2))]
    for copy in copies:
        copy.wait()
    total = g1[y]
    for d in range(len(copies)):
        total = total + rgy[d]
    g2[...] = total
    copies = [net.start(g2.at[t], rgx.at[d], 1, t) for d, (t, _) in enumerate(net.peers(1))]
    for copy in rows:
        copy.wait()
    rows = [net.start(left.at[:, c], left.at[:, c], 3, t) for t, _ in net.peers(3)]
    for copy in copies:
        copy.wait()
    total = g2[x]
    for d in range(len(copies)):
        total = total + rgx[d]
    g3[...] = total
    gz[z] = total
    copies = [net.start(g3, gz.at[z], 0, t) for t, _ in net.peers(0)]
    for copy in copies:
        copy.wait()
    total = gz[0]
    for d in range(1, dims[0]):
        total = total + gz[d]
    gram[c, y, x] = total
    for axis, view in ((1, gram.at[c, y, x]), (2, gram.at[c, y]), (3, gram.at[c])):
        copies = [net.start(view, view, axis, t) for t, _ in net.peers(axis)]
        for copy in copies:
            copy.wait()
    for copy in rows:
        copy.wait()


def ortho_kernel(gram, left, ortho, work, inverse):
    n = gram.shape[0]
    row = lax.broadcasted_iota(jnp.int32, (n, n), 0)
    col = lax.broadcasted_iota(jnp.int32, (n, n), 1)
    work[:, :n] = gram[...]
    work[:, n:] = jnp.where(row == col, 1.0, 0.0).astype(F32)
    ids = lax.broadcasted_iota(jnp.int32, (BLOCK, 2 * BLOCK), 0)
    lanes = lax.broadcasted_iota(jnp.int32, (BLOCK, BLOCK), 1)
    eye = jnp.where(lax.broadcasted_iota(jnp.int32, (BLOCK, BLOCK), 0) == lanes, 1.0, 0.0).astype(F32)
    for k in range(n // BLOCK):
        lo, hi = k * BLOCK, (k + 1) * BLOCK
        v = jnp.concatenate([work[lo:hi, lo:hi], eye], axis=1)
        for j in range(BLOCK):
            scale = lax.rsqrt(v[j : j + 1, j : j + 1])
            pivot = v[j : j + 1, :] * scale
            column = v[:, j : j + 1] * scale
            v = jnp.where(ids == j, pivot, v - jnp.where(ids > j, column * pivot, 0.0))
        upper = jnp.dot(v[:, BLOCK:], work[lo:hi, :], precision=HIGHEST, preferred_element_type=F32)
        inverse[lo:hi, :] = upper[:, n:]
        if hi < n:
            work[hi:, :] -= lax.dot_general(
                upper[:, hi:n], upper, (((0,), (0,)), ((), ())), precision=HIGHEST, preferred_element_type=F32
            )
    ortho[...] = lax.dot_general(
        left[...], inverse[...], (((1,), (1,)), ((), ())), precision=HIGHEST, preferred_element_type=F32
    )


def right_kernel(dims, part, out, sc, rc, acc, sya, rya, sxb, rxb, a2, b2, sxa, rxa, syb, ryb, a3, sz, rz, own, send, recv):
    net = Net(dims, send, recv)
    nz, nx, ny, nc = dims
    z, x, y, c = net.at
    half = part.shape[-1] // 2
    a, b = slice(0, half), slice(half, 2 * half)
    net.barrier()
    copies = []
    for i in range(nz):
        for d, (t, _) in enumerate(net.peers(3)):
            sc[d, i] = part[i, :, :, t].astype(BF16)
            copies.append(net.start(sc.at[d, i], rc.at[d, i], 3, t))
    for copy in copies:
        copy.wait()
    for i in range(nz):
        total = part[i, :, :, c]
        for d in range(nc - 1):
            total = total + rc[d, i].astype(F32)
        acc[i] = total
    copies = []
    for d, (t, _) in enumerate(net.peers(2)):
        sya[d] = acc[:, :, t, :, a].astype(BF16)
        copies.append(net.start(sya.at[d], rya.at[d], 2, t))
    for d, (t, _) in enumerate(net.peers(1)):
        sxb[d] = acc[:, t, :, :, b].astype(BF16)
        copies.append(net.start(sxb.at[d], rxb.at[d], 1, t))
    for copy in copies:
        copy.wait()
    total = acc[:, :, y, :, a]
    for d in range(ny - 1):
        total = total + rya[d].astype(F32)
    a2[...] = total
    total = acc[:, x, :, :, b]
    for d in range(nx - 1):
        total = total + rxb[d].astype(F32)
    b2[...] = total
    copies = []
    for d, (t, _) in enumerate(net.peers(1)):
        sxa[d] = a2[:, t].astype(BF16)
        copies.append(net.start(sxa.at[d], rxa.at[d], 1, t))
    for d, (t, _) in enumerate(net.peers(2)):
        syb[d] = b2[:, t].astype(BF16)
        copies.append(net.start(syb.at[d], ryb.at[d], 2, t))
    for copy in copies:
        copy.wait()
    total = a2[:, x]
    for d in range(nx - 1):
        total = total + rxa[d].astype(F32)
    a3[:, :, a] = total
    total = b2[:, y]
    for d in range(ny - 1):
        total = total + ryb[d].astype(F32)
    a3[:, :, b] = total
    copies = []
    for d, (t, _) in enumerate(net.peers(0)):
        sz[d] = a3[t].astype(BF16)
        copies.append(net.start(sz.at[d], rz.at[d], 0, t))
    for copy in copies:
        copy.wait()
    total = a3[z]
    for d in range(nz - 1):
        total = total + rz[d].astype(F32)
    mine = (total * (1.0 / (ny * nc))).astype(BF16)
    own[...] = mine
    out[z, x, y, c] = mine
    gather_all(net, own, out)


def call(kernel, dims, identity, operands, outs, scratch, local=False):
    vmem = pl.BlockSpec(memory_space=pltpu.VMEM)
    sems = [pltpu.SemaphoreType.DMA((MAX_COPIES,))] * 2
    if local:
        sems = sems + [pltpu.SemaphoreType.DMA]
    single = not isinstance(outs, tuple)
    return pl.pallas_call(
        functools.partial(kernel, dims),
        out_shape=outs,
        in_specs=[vmem] * len(operands),
        out_specs=vmem if single else (vmem,) * len(outs),
        scratch_shapes=[pltpu.VMEM(shape, kind) for shape, kind in scratch] + sems,
        compiler_params=pltpu.CompilerParams(
            collective_id=identity, has_side_effects=True, vmem_limit_bytes=48 << 20
        ),
    )(*operands)


def gather(dims, block, rows, rank):
    nz, nx, ny, nc = dims
    piece = rows // (ny * nc)
    full = call(
        gather_kernel, dims, 0, (block.reshape(ny, nc, piece, rank),),
        jax.ShapeDtypeStruct((nz, nx, ny, nc, piece, rank), BF16), [], local=True,
    )
    return full.reshape(rows * nz * nx, rank)


def sum_left(dims, part):
    nz, nx, ny, nc = dims
    rows, rank = part.shape
    piece = rows // (ny * nc)
    g = rank // (nc * ny * nx)
    pc, py, px = max(nc - 1, 1), max(ny - 1, 1), max(nx - 1, 1)
    left, gram = call(
        left_kernel, dims, 1, (part.reshape(ny, nc, piece, rank),),
        (jax.ShapeDtypeStruct((ny, nc, piece, rank), F32), jax.ShapeDtypeStruct((nc, ny, nx, g, rank), F32)),
        [
            ((pc, ny, piece, rank), F32), ((ny, piece, rank), F32), ((py, piece, rank), F32),
            ((nc, ny, nx, g, rank), F32), ((pc, ny, nx, g, rank), F32), ((ny, nx, g, rank), F32),
            ((py, nx, g, rank), F32), ((nx, g, rank), F32), ((px, g, rank), F32), ((g, rank), F32),
            ((nz, g, rank), F32),
        ],
    )
    return left.reshape(rows, rank), gram.reshape(rank, rank)


def sum_right(dims, part):
    nz, nx, ny, nc = dims
    width, rank = part.shape
    piece = width // (nz * nx * ny * nc)
    half = rank // 2
    pc, py, px, pz = max(nc - 1, 1), max(ny - 1, 1), max(nx - 1, 1), max(nz - 1, 1)
    two = lambda shape, kind: [(shape, kind), (shape, kind)]
    full = call(
        right_kernel, dims, 2, (part.reshape(nz, nx, ny, nc, piece, rank),),
        jax.ShapeDtypeStruct((nz, nx, ny, nc, piece, rank), BF16),
        two((pc, nz, nx, ny, piece, rank), BF16)
        + [((nz, nx, ny, piece, rank), F32)]
        + two((py, nz, nx, piece, half), BF16)
        + two((px, nz, ny, piece, half), BF16)
        + [((nz, nx, piece, half), F32), ((nz, ny, piece, half), F32)]
        + two((px, nz, piece, half), BF16)
        + two((py, nz, piece, half), BF16)
        + [((nz, piece, rank), F32)]
        + two((pz, piece, rank), BF16)
        + [((piece, rank), BF16)],
    )
    return full.reshape(width, rank)


def orthonormal(gram, left):
    rank = gram.shape[0]
    vmem = pl.BlockSpec(memory_space=pltpu.VMEM)
    return pl.pallas_call(
        ortho_kernel,
        out_shape=jax.ShapeDtypeStruct(left.shape, F32),
        in_specs=[vmem, vmem],
        out_specs=vmem,
        scratch_shapes=[pltpu.VMEM((rank, 2 * rank), F32), pltpu.VMEM((rank, rank), F32)],
        compiler_params=pltpu.CompilerParams(vmem_limit_bytes=32 << 20),
    )(gram, left)


def shards(dims, momentum, grad, right_prev):
    rows = grad.shape[2]
    width = grad.shape[3]
    rank = right_prev.shape[2]
    factor = width / math.sqrt(rank)
    buffer = momentum[0, 0].astype(F32) + grad[0, 0].astype(F32)
    buffer_b = buffer.astype(BF16)
    local_left = jnp.dot(buffer_b, gather(dims, right_prev[0], rows, rank), preferred_element_type=F32)
    summed, gram = sum_left(dims, local_left)
    ortho = orthonormal(gram, summed)
    ortho_b = ortho.astype(BF16)
    part = lax.dot_general(buffer_b, ortho_b, (((0,), (0,)), ((), ())), preferred_element_type=F32)
    right_full = sum_right(dims, part)
    wide = right_full.astype(F32)
    norms = jnp.sqrt(jnp.sum(wide * wide, axis=0) + epsilon_norm)
    right_own = lax.dynamic_slice_in_dim(right_full, lax.axis_index("shard") * rows, rows, axis=0)
    scaled = (ortho * (factor / norms)).astype(BF16)
    feedback = lax.dot_general(ortho_b, right_full, (((1,), (1,)), ((), ())), preferred_element_type=F32)
    momentum_new = (buffer - (1.0 - momentum_decay) * feedback).astype(BF16)
    stepped = lax.dot_general(scaled, right_full, (((1,), (1,)), ((), ())), preferred_element_type=F32)
    return momentum_new[None, None], stepped.astype(BF16)[None], right_own[None]


def solution(mesh):
    dims = grid_of(mesh.shape["shard"], mesh.shape["replica"])
    return jax.shard_map(
        functools.partial(shards, dims),
        mesh=mesh,
        in_specs=(
            P(None, "replica", "shard", None),
            P(None, "replica", "shard", None),
            P(None, "shard", None),
        ),
        out_specs=(
            P(None, "replica", "shard", None),
            P(None, "shard", None),
            P(None, "shard", None),
        ),
        check_vma=False,
    )
```

time: 440 us -> 161 us (0.37)
  waiting for transfers between devices: 310 us -> 0 us
  Pallas kernels: 0 us -> 129 us
  other arithmetic: 56.5 us -> 8.13 us
  blocking collectives: 21.5 us -> 0 us
  matrix products: 29.9 us -> 14 us
  between operations: 15.5 us -> 0.7 us
    psum x3 -> x0, waiting for transfers between devices: 139 us -> none  [the longest x1 71.9 us: shards(): lax.psum(jnp.dot(summed.T, summed, precision=lax.Precision.HIGHEST), 'sha...]
    pallas_call x0 -> x4, Pallas kernels: none -> 129 us  [the longest x3 102 us: call(): pl.pallas_call(functools.partial(kernel, dims), out_shape=outs, in_specs=...]
    reduce_scatter x1 -> x0, waiting for transfers between devices: 88 us -> none  [shards(): lax.psum_scatter(project(jnp.int32(0), rows * lax.axis_size('shard')), 's...]
    all_gather x2 -> x0, waiting for transfers between devices: 82.5 us -> none  [the longest x1 54 us: shards(): lax.all_gather(right_prev[0], 'shard', axis=0, tiled=True)]
    another operation x9 -> x0, other arithmetic: 53.7 us -> none  [the longest x6 34 us: orthonormal(): chol = jnp.linalg.cholesky(gram)]
    psum x1 -> x0, blocking collectives: 21.5 us -> none  [shards(): squares = lax.psum(jnp.sum(right_part * right_part, axis=0), 'shard')]
    dot_general x3 -> x2, matrix products: 16.6 us -> 6.71 us  [the longest x1 5.46 us: shards(): lax.dot_general(buffer_b, ortho_b, (((0,), (0,)), ((), ())), preferred_el...]
    convert_element_type x0 -> x1, other arithmetic: none -> 7.54 us  [shards(): buffer_b = buffer.astype(BF16)]
  transfers between devices with their start and end apart: 6 -> 0, of which waited for: 6 -> 0; matrix products, arithmetic and copies ran while one was open for 0% -> 0% of each run, Pallas kernels for 0% -> 0%
where the time goes in v1:
time: 161 us; the launch traced here: 160 us
  Pallas kernels  129 us (80%)
  matrix products  14 us (9%)
  other arithmetic  8.13 us (5%)
  local copies, waits for them, and re-layouts  7.98 us (5%)
    pallas_call x3, Pallas kernels, call(): pl.pallas_call(functools.partial(kernel, dims), out_shape=outs, in_specs=...  102 us
    pallas_call x1, Pallas kernels, orthonormal(): pl.pallas_call(ortho_kernel, out_shape=jax.ShapeDtypeStruct(left.shape, F...  27.1 us
    convert_element_type x1, other arithmetic, shards(): buffer_b = buffer.astype(BF16)  7.54 us
    dot_general x1, local copies, waits for them, and re-layouts, shards(): lax.dot_general(buffer_b, ortho_b, (((0,), (0,)), ((), ())), preferred_el...  6.41 us
    dot_general x1, matrix products, shards(): lax.dot_general(buffer_b, ortho_b, (((0,), (0,)), ((), ())), preferred_el...  5.46 us
    dot_general x1, matrix products, shards(): lax.dot_general(ortho_b, right_full, (((1,), (1,)), ((), ())), preferred_...  3.98 us
    dot_general x1, matrix products, shards(): lax.dot_general(scaled, right_full, (((1,), (1,)), ((), ())), preferred_e...  3.34 us

profile of v1, /device:TPU:0, one launch (start us, length us, event | category | flops | bytes accessed | tf_op | source)
XLA Modules:
  0.0 160.2 jit_solution(1401544825951556682)
XLA Ops:
  0.6 0.0 copy-start
  0.6 7.5 %fusion.1 = (bf16[1,1,512,4096]{3,2,1,0:T(8,128)(2,1)S(1)}, bf16[4096,512]{0,1:T(8,128)(2,1)}) fusion(bf16[1,1,512,4096]{3,2,1,0:T(8,128)(2,1)} %param.4, bf16[1,1,512,4096]{3,2,1,0:T(8,128)(2,1)} %param.3), kind=kLoop, calls=%fused_computation.4 | loop fusion | flops 10485760 | bytes 16777216 | tf_op jit(solution)/shard_map/convert_element_type | solution.py:367
  8.2 0.0 copy-done
  8.2 25.7 %shard_map.58 = bf16[4,2,2,2,128,256]{5,4,3,2,1,0:T(8,128)(2,1)S(1)} custom-call(bf16[2,2,128,256]{3,2,1,0:T(8,128)(2,1)S(1)} %bitcast.43), custom_call_target="tpu_custom_call" | custom-call | tf_op jit(solution)/shard_map/pallas_call | solution.py:283
  33.9 1.2 fusion.10.part
  35.1 30.5 %shard_map.59 = (f32[2,2,128,256]{3,2,1,0:T(8,128)S(1)}, f32[2,2,2,32,256]{4,3,2,1,0:T(8,128)S(1)}) custom-call(f32[2,2,128,256]{3,2,1,0:T(8,128)S(1)} %fusion.10.part), custom_call_target="tpu_custom_call" | custom-call | tf_op jit(solution)/shard_map/pallas_call | solution.py:283
  65.6 27.1 %shard_map.60 = f32[512,256]{1,0:T(8,128)S(1)} custom-call(f32[256,256]{1,0:T(8,128)S(1)} %bitcast.44, f32[512,256]{1,0:T(8,128)S(1)} %bitcast.42), custom_call_target="tpu_custom_call" | custom-call | tf_op jit(solution)/shard_map/pallas_call | solution.py:351
  92.7 6.4 %copy.9 = bf16[4096,512]{1,0:T(8,128)(2,1)} copy(bf16[4096,512]{0,1:T(8,128)(2,1)} %get-tuple-element.8) | data formatting | bytes 8388608 | tf_op jit(solution)/shard_map/dot_general | solution.py:372
  99.1 5.5 %fusion.5.part = f32[4,2,2,2,128,256]{5,4,3,2,1,0:T(8,128)} fusion(bf16[4,2,2,2,128,512]{5,4,3,2,1,0:T(8,128)(2,1)} %bitcast.45, f32[512,256]{1,0:T(8,128)S(1)} %shard_map.60), kind=kOutput, calls=%fused_computation.11 | convolution fusion | flops 1073872896 | bytes 8912896 | tf_op jit(solution)/shard_map/dot_general | solution.py:372
  104.5 46.2 %shard_map.61 = bf16[4,2,2,2,128,256]{5,4,3,2,1,0:T(8,128)(2,1)S(1)} custom-call(f32[4,2,2,2,128,256]{5,4,3,2,1,0:T(8,128)} %fusion.5.part), custom_call_target="tpu_custom_call" | custom-call | tf_op jit(solution)/shard_map/pallas_call | solution.py:283
  150.7 0.0 copy-start.1
  150.7 0.0 copy-start.2
  150.7 0.6 multiply_reduce_fusion
  151.3 3.3 %fusion.2 = bf16[1,512,4096]{2,1,0:T(8,128)(2,1)} fusion(bf16[4096,256]{1,0:T(8,128)(2,1)S(1)} %bitcast.38, f32[512,256]{1,0:T(8,128)S(1)} %shard_map.60, f32[256]{0:T(256)S(1)} %rsqrt_multiply_fusion), kind=kOutput, calls=%fused_computation.6 | convolution fusion | flops 1076101120 | bytes 6816768 | tf_op jit(solution)/shard_map/dot_general | solution.py:380
  154.7 0.0 copy-done.1
  154.7 0.8 copy-done.2
  155.5 4.0 %fusion.3 = bf16[1,1,512,4096]{3,2,1,0:T(8,128)(2,1)} fusion(bf16[4096,256]{1,0:T(8,128)(2,1)S(1)} %bitcast.39, bf16[1,1,512,4096]{3,2,1,0:T(8,128)(2,1)S(1)} %copy-done.1, bf16[1,1,512,4096]{3,2,1,0:T(8,128)(2,1)S(1)} %copy-done.2, f32[512,256]{1,0:T(8,128)S(1)} %shard_map.60), kind=kOutput, calls=%fused_computation.7 | convolution fusion | flops 1086455808 | bytes 15204352 | tf_op jit(solution)/shard_map/dot_general | solution.py:378
  159.5 0.7 dynamic-slice_bitcast_fusion
  (1 shorter events, 0.0 us)
Async XLA Ops:
  0.6 7.6 %copy-start = (bf16[1,512,256]{2,1,0:T(8,128)(2,1)S(1)}, bf16[1,512,256]{2,1,0:T(8,128)(2,1)}, u32[]{:S(2)}) copy-start(bf16[1,512,256]{2,1,0:T(8,128)(2,1)} %param.5) | copy-start | bytes 786436
  150.7 4.0 %copy-start.1 = (bf16[1,1,512,4096]{3,2,1,0:T(8,128)(2,1)S(1)}, bf16[1,1,512,4096]{3,2,1,0:T(8,128)(2,1)}, u32[]{:S(2)}) copy-start(bf16[1,1,512,4096]{3,2,1,0:T(8,128)(2,1)} %param.4) | copy-start | bytes 12582916
  150.7 4.8 %copy-start.2 = (bf16[1,1,512,4096]{3,2,1,0:T(8,128)(2,1)S(1)}, bf16[1,1,512,4096]{3,2,1,0:T(8,128)(2,1)}, u32[]{:S(2)}) copy-start(bf16[1,1,512,4096]{3,2,1,0:T(8,128)(2,1)} %param.3) | copy-start | bytes 12582916

commit v2 on v1

--- a/solution.py
+++ b/solution.py
@@ -14,7 +14,9 @@
 HIGHEST = lax.Precision.HIGHEST
 F32 = jnp.float32
 BF16 = jnp.bfloat16
-BLOCK = 32
+BLOCK = 64
+PIVOTS = 4
+CHUNKS = 8
 MAX_COPIES = 96
 
 
@@ -71,10 +73,10 @@
         return copy
 
 
-def gather_all(net, own, out):
+def gather_all(net, own, out, work=None):
     z, x, y, c = net.at
-    half = out.shape[-1] // 2
-    a, b = pl.ds(0, half), pl.ds(half, half)
+    half = out.shape[0] // 2
+    a, b = pl.ds(0, half), pl.ds(half, out.shape[0] - half)
     others = net.peers(3)
     sent = []
 
@@ -85,18 +87,20 @@
     first = [(net.start(own, out.at[z, x, y, c], 0, t), f) for t, f in net.peers(0)]
     for oc, _ in others:
         sent.append(net.start(own, out.at[z, x, y, c], 3, oc))
+    if work is not None:
+        work()
     for copy, f in first:
         copy.wait()
     for copy, f in first:
         forward(out.at[f, x, y, c])
-    mine_a, mine_b = out.at[:, x, y, c, :, a], out.at[:, x, y, c, :, b]
-    second = [(net.start(mine_a, mine_a, 1, t), out.at[:, f, y, c, :, a]) for t, f in net.peers(1)]
-    second += [(net.start(mine_b, mine_b, 2, t), out.at[:, x, f, c, :, b]) for t, f in net.peers(2)]
+    mine_a, mine_b = out.at[a, x, y, c], out.at[b, x, y, c]
+    second = [(net.start(mine_a, mine_a, 1, t), out.at[a, f, y, c]) for t, f in net.peers(1)]
+    second += [(net.start(mine_b, mine_b, 2, t), out.at[b, x, f, c]) for t, f in net.peers(2)]
     for copy, _ in second:
         copy.wait()
-    mine_a, mine_b = out.at[:, :, y, c, :, a], out.at[:, x, :, c, :, b]
-    third = [(net.start(mine_a, mine_a, 2, t), out.at[:, :, f, c, :, a]) for t, f in net.peers(2)]
-    third += [(net.start(mine_b, mine_b, 1, t), out.at[:, f, :, c, :, b]) for t, f in net.peers(1)]
+    mine_a, mine_b = out.at[a, :, y, c], out.at[b, x, :, c]
+    third = [(net.start(mine_a, mine_a, 2, t), out.at[a, :, f, c]) for t, f in net.peers(2)]
+    third += [(net.start(mine_b, mine_b, 1, t), out.at[b, f, :, c]) for t, f in net.peers(1)]
     for _, view in second:
         forward(view)
     for copy, _ in third:
@@ -107,14 +111,32 @@
         copy.wait()
 
 
-def gather_kernel(dims, block, out, send, recv, local):
+def gather_kernel(dims, block, momentum, grad, out, buffer, m, g, send, recv, local):
     net = Net(dims, send, recv)
     z, x, y, c = net.at
-    own = pltpu.make_async_copy(block.at[y, c], out.at[z, x, y, c], local)
+    own = pltpu.make_async_copy(block.at[y, c], out.at[z, x, y, c], local.at[0])
     own.start()
+    loads = []
+    for k in range(CHUNKS):
+        size = buffer.shape[0] // CHUNKS
+        rows = pl.ds(k * size, size)
+        pair = [
+            pltpu.make_async_copy(momentum.at[rows], m.at[rows], local.at[2 * k + 1]),
+            pltpu.make_async_copy(grad.at[rows], g.at[rows], local.at[2 * k + 2]),
+        ]
+        for copy in pair:
+            copy.start()
+        loads.append((rows, pair))
     net.barrier()
     own.wait()
-    gather_all(net, block.at[y, c], out)
+
+    def add():
+        for rows, pair in loads:
+            for copy in pair:
+                copy.wait()
+            buffer[rows, :] = (m[rows, :].astype(F32) + g[rows, :].astype(F32)).astype(BF16)
+
+    gather_all(net, block.at[y, c], out, add)
 
 
 def left_kernel(dims, part, left, gram, rc, acc, ry, g, rgc, g1, rgy, g2, rgx, g3, gz, send, recv):
@@ -178,43 +200,89 @@
         copy.wait()
 
 
-def ortho_kernel(gram, left, ortho, work, inverse):
+def factor_inverse(block):
+    n = block.shape[0]
+    row = lax.broadcasted_iota(jnp.int32, (8, n), 0)
+    lane = lax.broadcasted_iota(jnp.int32, (8, n), 1)
+    parts = [
+        jnp.concatenate([block[8 * i : 8 * i + 8, :], jnp.where(lane == row + 8 * i, 1.0, 0.0).astype(F32)], axis=1)
+        for i in range(n // 8)
+    ]
+    ids = lax.broadcasted_iota(jnp.int32, (8, 2 * n), 0)
+    for j in range(0, n, PIVOTS):
+        first, o = j // 8, j % 8
+        head = parts[first]
+        s = {}
+        for p in range(PIVOTS):
+            for q in range(p, PIVOTS):
+                s[p, q] = jnp.broadcast_to(head[o + p : o + p + 1, j + q : j + q + 1], (1, 2 * n))
+        rows = [head[o + p : o + p + 1, :] for p in range(PIVOTS)]
+        cols = [
+            [jnp.broadcast_to(part[:, j + p : j + p + 1], (8, 2 * n)) for part in parts[first:]]
+            for p in range(PIVOTS)
+        ]
+        total = None
+        done = []
+        for p in range(PIVOTS):
+            r = lax.rsqrt(s[p, p])
+            inv = r * r
+            for q in range(p + 1, PIVOTS):
+                t = s[p, q] * inv
+                rows[q] = rows[q] - t * rows[p]
+                cols[q] = [cq - t * cp for cq, cp in zip(cols[q], cols[p])]
+                for w in range(q, PIVOTS):
+                    s[q, w] = s[q, w] - t * s[p, w]
+            done.append(rows[p] * r)
+            scaled = rows[p] * inv
+            terms = [cp * scaled for cp in cols[p]]
+            total = terms if total is None else [u + v for u, v in zip(total, terms)]
+        head = jnp.where(ids >= o + PIVOTS, head - total[0], head)
+        for p in range(PIVOTS):
+            head = jnp.where(ids == o + p, done[p], head)
+        rest = [part - u for part, u in zip(parts[first + 1 :], total[1:])]
+        parts = parts[:first] + [head] + rest
+    return jnp.concatenate(parts, axis=0)[:, n:]
+
+
+def ortho_kernel(gram, left, ortho, rounded, work, inverse):
     n = gram.shape[0]
     row = lax.broadcasted_iota(jnp.int32, (n, n), 0)
     col = lax.broadcasted_iota(jnp.int32, (n, n), 1)
     work[:, :n] = gram[...]
     work[:, n:] = jnp.where(row == col, 1.0, 0.0).astype(F32)
-    ids = lax.broadcasted_iota(jnp.int32, (BLOCK, 2 * BLOCK), 0)
-    lanes = lax.broadcasted_iota(jnp.int32, (BLOCK, BLOCK), 1)
-    eye = jnp.where(lax.broadcasted_iota(jnp.int32, (BLOCK, BLOCK), 0) == lanes, 1.0, 0.0).astype(F32)
-    for k in range(n // BLOCK):
-        lo, hi = k * BLOCK, (k + 1) * BLOCK
-        v = jnp.concatenate([work[lo:hi, lo:hi], eye], axis=1)
-        for j in range(BLOCK):
-            scale = lax.rsqrt(v[j : j + 1, j : j + 1])
-            pivot = v[j : j + 1, :] * scale
-            column = v[:, j : j + 1] * scale
-            v = jnp.where(ids == j, pivot, v - jnp.where(ids > j, column * pivot, 0.0))
-        upper = jnp.dot(v[:, BLOCK:], work[lo:hi, :], precision=HIGHEST, preferred_element_type=F32)
-        inverse[lo:hi, :] = upper[:, n:]
+    inverse[...] = jnp.zeros((n, n), F32)
+    for lo in range(0, n, BLOCK):
+        hi = lo + BLOCK
+        start, end = hi // 128 * 128, (n + hi + 127) // 128 * 128
+        corner = factor_inverse(work[lo:hi, lo:hi])
+        upper = jnp.dot(corner, work[lo:hi, start:end], precision=HIGHEST, preferred_element_type=F32)
+        inverse[lo:hi, : end - n] = upper[:, n - start :]
         if hi < n:
-            work[hi:, :] -= lax.dot_general(
-                upper[:, hi:n], upper, (((0,), (0,)), ((), ())), precision=HIGHEST, preferred_element_type=F32
+            work[hi:, start:end] -= lax.dot_general(
+                upper[:, hi - start : n - start], upper, (((0,), (0,)), ((), ())),
+                precision=HIGHEST, preferred_element_type=F32,
             )
-    ortho[...] = lax.dot_general(
+    result = lax.dot_general(
         left[...], inverse[...], (((1,), (1,)), ((), ())), precision=HIGHEST, preferred_element_type=F32
     )
-
-
-def right_kernel(dims, part, out, sc, rc, acc, sya, rya, sxb, rxb, a2, b2, sxa, rxa, syb, ryb, a3, sz, rz, own, send, recv):
+    ortho[...] = result
+    rounded[...] = result.astype(BF16)
+
+
+def right_kernel(dims, buffer, ortho, out, part, sc, rc, acc, sya, rya, sxb, rxb, a2, b2, sxa, rxa, syb, ryb, a3, sz, rz, own, send, recv):
     net = Net(dims, send, recv)
     nz, nx, ny, nc = dims
     z, x, y, c = net.at
-    half = part.shape[-1] // 2
-    a, b = slice(0, half), slice(half, 2 * half)
+    half = nz // 2
+    a, b = slice(0, half), slice(half, nz)
     net.barrier()
     copies = []
+    wide = buffer.shape[1] // nz
     for i in range(nz):
+        product = lax.dot_general(
+            buffer[:, i * wide : (i + 1) * wide], ortho[...], (((0,), (0,)), ((), ())), preferred_element_type=F32
+        )
+        part[i] = product.reshape(part.shape[1:])
         for d, (t, _) in enumerate(net.peers(3)):
             sc[d, i] = part[i, :, :, t].astype(BF16)
             copies.append(net.start(sc.at[d, i], rc.at[d, i], 3, t))
@@ -227,18 +295,18 @@
         acc[i] = total
     copies = []
     for d, (t, _) in enumerate(net.peers(2)):
-        sya[d] = acc[:, :, t, :, a].astype(BF16)
+        sya[d] = acc[a, :, t].astype(BF16)
         copies.append(net.start(sya.at[d], rya.at[d], 2, t))
     for d, (t, _) in enumerate(net.peers(1)):
-        sxb[d] = acc[:, t, :, :, b].astype(BF16)
+        sxb[d] = acc[b, t].astype(BF16)
         copies.append(net.start(sxb.at[d], rxb.at[d], 1, t))
     for copy in copies:
         copy.wait()
-    total = acc[:, :, y, :, a]
+    total = acc[a, :, y]
     for d in range(ny - 1):
         total = total + rya[d].astype(F32)
     a2[...] = total
-    total = acc[:, x, :, :, b]
+    total = acc[b, x]
     for d in range(nx - 1):
         total = total + rxb[d].astype(F32)
     b2[...] = total
@@ -254,11 +322,11 @@
     total = a2[:, x]
     for d in range(nx - 1):
         total = total + rxa[d].astype(F32)
-    a3[:, :, a] = total
+    a3[a] = total
     total = b2[:, y]
     for d in range(ny - 1):
         total = total + ryb[d].astype(F32)
-    a3[:, :, b] = total
+    a3[b] = total
     copies = []
     for d, (t, _) in enumerate(net.peers(0)):
         sz[d] = a3[t].astype(BF16)
@@ -274,16 +342,17 @@
     gather_all(net, own, out)
 
 
-def call(kernel, dims, identity, operands, outs, scratch, local=False):
+def call(kernel, dims, identity, operands, outs, scratch, local=0):
     vmem = pl.BlockSpec(memory_space=pltpu.VMEM)
+    rest = pl.BlockSpec(memory_space=pltpu.MemorySpace.HBM)
     sems = [pltpu.SemaphoreType.DMA((MAX_COPIES,))] * 2
     if local:
-        sems = sems + [pltpu.SemaphoreType.DMA]
+        sems = sems + [pltpu.SemaphoreType.DMA((local,))]
     single = not isinstance(outs, tuple)
     return pl.pallas_call(
         functools.partial(kernel, dims),
         out_shape=outs,
-        in_specs=[vmem] * len(operands),
+        in_specs=[vmem] + [rest if local else vmem] * (len(operands) - 1),
         out_specs=vmem if single else (vmem,) * len(outs),
         scratch_shapes=[pltpu.VMEM(shape, kind) for shape, kind in scratch] + sems,
         compiler_params=pltpu.CompilerParams(
@@ -292,14 +361,16 @@
     )(*operands)
 
 
-def gather(dims, block, rows, rank):
+def gather(dims, block, momentum, grad):
     nz, nx, ny, nc = dims
+    rows, rank = block.shape
     piece = rows // (ny * nc)
-    full = call(
-        gather_kernel, dims, 0, (block.reshape(ny, nc, piece, rank),),
-        jax.ShapeDtypeStruct((nz, nx, ny, nc, piece, rank), BF16), [], local=True,
+    full, buffer_b = call(
+        gather_kernel, dims, 0, (block.reshape(ny, nc, piece, rank), momentum, grad),
+        (jax.ShapeDtypeStruct((nz, nx, ny, nc, piece, rank), BF16), jax.ShapeDtypeStruct(momentum.shape, BF16)),
+        [(momentum.shape, BF16), (momentum.shape, BF16)], local=2 * CHUNKS + 1,
     )
-    return full.reshape(rows * nz * nx, rank)
+    return full.reshape(rows * nz * nx, rank), buffer_b
 
 
 def sum_left(dims, part):
@@ -321,23 +392,25 @@
     return left.reshape(rows, rank), gram.reshape(rank, rank)
 
 
-def sum_right(dims, part):
+def sum_right(dims, buffer_b, ortho_b):
     nz, nx, ny, nc = dims
-    width, rank = part.shape
+    width, rank = buffer_b.shape[1], ortho_b.shape[1]
     piece = width // (nz * nx * ny * nc)
-    half = rank // 2
+    low = nz // 2
+    high = nz - low
     pc, py, px, pz = max(nc - 1, 1), max(ny - 1, 1), max(nx - 1, 1), max(nz - 1, 1)
     two = lambda shape, kind: [(shape, kind), (shape, kind)]
     full = call(
-        right_kernel, dims, 2, (part.reshape(nz, nx, ny, nc, piece, rank),),
+        right_kernel, dims, 2, (buffer_b, ortho_b),
         jax.ShapeDtypeStruct((nz, nx, ny, nc, piece, rank), BF16),
-        two((pc, nz, nx, ny, piece, rank), BF16)
+        [((nz, nx, ny, nc, piece, rank), F32)]
+        + two((pc, nz, nx, ny, piece, rank), BF16)
         + [((nz, nx, ny, piece, rank), F32)]
-        + two((py, nz, nx, piece, half), BF16)
-        + two((px, nz, ny, piece, half), BF16)
-        + [((nz, nx, piece, half), F32), ((nz, ny, piece, half), F32)]
-        + two((px, nz, piece, half), BF16)
-        + two((py, nz, piece, half), BF16)
+        + two((py, low, nx, piece, rank), BF16)
+        + two((px, high, ny, piece, rank), BF16)
+        + [((low, nx, piece, rank), F32), ((high, ny, piece, rank), F32)]
+        + two((px, low, piece, rank), BF16)
+        + two((py, high, piece, rank), BF16)
         + [((nz, piece, rank), F32)]
         + two((pz, piece, rank), BF16)
         + [((piece, rank), BF16)],
@@ -350,9 +423,9 @@
     vmem = pl.BlockSpec(memory_space=pltpu.VMEM)
     return pl.pallas_call(
         ortho_kernel,
-        out_shape=jax.ShapeDtypeStruct(left.shape, F32),
+        out_shape=(jax.ShapeDtypeStruct(left.shape, F32), jax.ShapeDtypeStruct(left.shape, BF16)),
         in_specs=[vmem, vmem],
-        out_specs=vmem,
+        out_specs=(vmem, vmem),
         scratch_shapes=[pltpu.VMEM((rank, 2 * rank), F32), pltpu.VMEM((rank, rank), F32)],
         compiler_params=pltpu.CompilerParams(vmem_limit_bytes=32 << 20),
     )(gram, left)
@@ -364,13 +437,11 @@
     rank = right_prev.shape[2]
     factor = width / math.sqrt(rank)
     buffer = momentum[0, 0].astype(F32) + grad[0, 0].astype(F32)
-    buffer_b = buffer.astype(BF16)
-    local_left = jnp.dot(buffer_b, gather(dims, right_prev[0], rows, rank), preferred_element_type=F32)
+    prev_full, buffer_b = gather(dims, right_prev[0], momentum[0, 0], grad[0, 0])
+    local_left = jnp.dot(buffer_b, prev_full, preferred_element_type=F32)
     summed, gram = sum_left(dims, local_left)
-    ortho = orthonormal(gram, summed)
-    ortho_b = ortho.astype(BF16)
-    part = lax.dot_general(buffer_b, ortho_b, (((0,), (0,)), ((), ())), preferred_element_type=F32)
-    right_full = sum_right(dims, part)
+    ortho, ortho_b = orthonormal(gram, summed)
+    right_full = sum_right(dims, buffer_b, ortho_b)
     wide = right_full.astype(F32)
     norms = jnp.sqrt(jnp.sum(wide * wide, axis=0) + epsilon_norm)
     right_own = lax.dynamic_slice_in_dim(right_full, lax.axis_index("shard") * rows, rows, axis=0)

time: 161 us -> 133 us (0.83)
  Pallas kernels: 129 us -> 118 us
  other arithmetic: 8.13 us -> 0.59 us
  local copies, waits for them, and re-layouts: 7.98 us -> 2.49 us
  matrix products: 14 us -> 10.7 us
    pallas_call x1, Pallas kernels: 27.1 us -> 11.8 us  [orthonormal(): pl.pallas_call(ortho_kernel, out_shape=(jax.ShapeDtypeStruct(left.shape,...]
    convert_element_type x1 -> x0, other arithmetic: 7.54 us -> none  [shards(): buffer_b = buffer.astype(BF16)]
    dot_general x1 -> x0, local copies, waits for them, and re-layouts: 6.41 us -> none  [shards(): lax.dot_general(buffer_b, ortho_b, (((0,), (0,)), ((), ())), preferred_el...]
    pallas_call x3, Pallas kernels: 102 us -> 107 us  [call(): pl.pallas_call(functools.partial(kernel, dims), out_shape=outs, in_specs=...]
    dot_general x2 -> x1, matrix products: 6.71 us -> 3.44 us  [shards(): local_left = jnp.dot(buffer_b, prev_full, preferred_element_type=F32)]
where the time goes in v2:
time: 133 us
  Pallas kernels  118 us (89%)
  matrix products  10.7 us (8%)
  local copies, waits for them, and re-layouts  2.49 us (2%)
    pallas_call x3, Pallas kernels, call(): pl.pallas_call(functools.partial(kernel, dims), out_shape=outs, in_specs=...  107 us
    pallas_call x1, Pallas kernels, orthonormal(): pl.pallas_call(ortho_kernel, out_shape=(jax.ShapeDtypeStruct(left.shape,...  11.8 us
    dot_general x1, matrix products, shards(): lax.dot_general(ortho_b, right_full, (((1,), (1,)), ((), ())), preferred_...  3.96 us
    dot_general x1, matrix products, shards(): local_left = jnp.dot(buffer_b, prev_full, preferred_element_type=F32)  3.44 us
    dot_general x1, matrix products, shards(): lax.dot_general(scaled, right_full, (((1,), (1,)), ((), ())), preferred_e...  3.34 us

profile of v2, /device:TPU:0, one launch (start us, length us, event | category | flops | bytes accessed | tf_op | source)
XLA Modules:
  0.0 132.8 jit_solution(7414482125534380193)
XLA Ops:
  0.6 0.0 copy-start
  0.6 0.9 copy-done
  1.6 27.8 %shard_map.58 = (bf16[4,2,2,2,128,256]{5,4,3,2,1,0:T(8,128)(2,1)S(1)}, bf16[512,4096]{1,0:T(8,128)(2,1)}) custom-call(bf16[2,2,128,256]{3,2,1,0:T(8,128)(2,1)S(1)} %bitcast.29, bf16[512,4096]{1,0:T(8,128)(2,1)} %bitcast.32, bf16[512,4096]{1,0:T(8,128)(2,1)} %bitcast.33), custom_call_target="tpu_custom_call" | custom-call | tf_op jit(solution)/shard_map/pallas_call | solution.py:352
  29.4 3.4 %fusion.3.part = f32[2,2,128,256]{3,2,1,0:T(8,128)S(1)} fusion(bf16[2,2,128,4096]{3,2,1,0:T(8,128)(2,1)} %bitcast.34, bf16[4096,256,1,1]{1,0,3,2:T(8,128)(2,1)S(1)} %bitcast.31), kind=kOutput, calls=%fused_computation.9 | convolution fusion | flops 1073741824 | bytes 6815744 | tf_op jit(solution)/shard_map/dot_general | solution.py:441
  32.8 30.5 %shard_map.59 = (f32[2,2,128,256]{3,2,1,0:T(8,128)S(1)}, f32[2,2,2,32,256]{4,3,2,1,0:T(8,128)S(1)}) custom-call(f32[2,2,128,256]{3,2,1,0:T(8,128)S(1)} %fusion.3.part), custom_call_target="tpu_custom_call" | custom-call | tf_op jit(solution)/shard_map/pallas_call | solution.py:352
  63.3 11.8 %shard_map.60 = (f32[512,256]{1,0:T(8,128)S(1)}, bf16[512,256]{1,0:T(8,128)(2,1)S(1)}) custom-call(f32[256,256]{1,0:T(8,128)S(1)} %bitcast.30, f32[512,256]{1,0:T(8,128)S(1)} %bitcast.28), custom_call_target="tpu_custom_call" | custom-call | tf_op jit(solution)/shard_map/pallas_call | solution.py:424
  75.1 48.3 %shard_map.61 = bf16[4,2,2,2,128,256]{5,4,3,2,1,0:T(8,128)(2,1)S(1)} custom-call(bf16[512,4096]{1,0:T(8,128)(2,1)} %get-tuple-element.9.buffer, bf16[512,256]{1,0:T(8,128)(2,1)S(1)} %get-tuple-element.13.ortho), custom_call_target="tpu_custom_call" | custom-call | tf_op jit(solution)/shard_map/pallas_call | solution.py:352
  123.3 0.0 copy-start.1
  123.4 0.0 copy-start.2
  123.4 0.6 multiply_reduce_fusion
  124.0 3.3 %fusion = bf16[1,512,4096]{2,1,0:T(8,128)(2,1)} fusion(bf16[4096,256]{1,0:T(8,128)(2,1)S(1)} %bitcast.25, f32[512,256]{1,0:T(8,128)S(1)} %get-tuple-element.14, f32[256]{0:T(256)S(1)} %rsqrt_multiply_fusion), kind=kOutput, calls=%fused_computation.2 | convolution fusion | flops 1076101120 | bytes 6816768 | tf_op jit(solution)/shard_map/dot_general | solution.py:451
  127.3 0.0 copy-done.1
  127.3 0.8 copy-done.2
  128.1 4.0 %fusion.1 = bf16[1,1,512,4096]{3,2,1,0:T(8,128)(2,1)} fusion(bf16[512,256]{1,0:T(8,128)(2,1)S(1)} %get-tuple-element.13.ortho, bf16[4096,256]{1,0:T(8,128)(2,1)S(1)} %bitcast.26, bf16[1,1,512,4096]{3,2,1,0:T(8,128)(2,1)S(1)} %copy-done.2, bf16[1,1,512,4096]{3,2,1,0:T(8,128)(2,1)S(1)} %copy-done.1), kind=kOutput, calls=%fused_computation.3 | convolution fusion | flops 1086324736 | bytes 14942208 | tf_op jit(solution)/shard_map/dot_general | solution.py:449
  132.1 0.7 dynamic-slice_bitcast_fusion
  (1 shorter events, 0.0 us)
Async XLA Ops:
  0.6 1.0 copy-start
  123.3 4.0 %copy-start.1 = (bf16[1,1,512,4096]{3,2,1,0:T(8,128)(2,1)S(1)}, bf16[1,1,512,4096]{3,2,1,0:T(8,128)(2,1)}, u32[]{:S(2)}) copy-start(bf16[1,1,512,4096]{3,2,1,0:T(8,128)(2,1)} %param.3) | copy-start | bytes 12582916
  123.4 4.8 %copy-start.2 = (bf16[1,1,512,4096]{3,2,1,0:T(8,128)(2,1)S(1)}, bf16[1,1,512,4096]{3,2,1,0:T(8,128)(2,1)}, u32[]{:S(2)}) copy-start(bf16[1,1,512,4096]{3,2,1,0:T(8,128)(2,1)} %param.4) | copy-start | bytes 12582916

commit v3 on v2

v3 whole, which is shorter than its diff:
```python
import functools
import math

import jax
import jax.numpy as jnp
from jax import lax
from jax.experimental import pallas as pl
from jax.experimental.pallas import tpu as pltpu
from jax.sharding import PartitionSpec as P

momentum_decay = 0.95
epsilon_norm = 1e-06
MESH = pl.DeviceIdType.MESH
HIGHEST = lax.Precision.HIGHEST
F32 = jnp.float32
BF16 = jnp.bfloat16
BLOCK = 64
PIVOTS = 4
CHUNKS = 8


def grid_of(shards_n, replicas_n):
    x = math.isqrt(shards_n // 2)
    if x < 1 or 2 * x * x != shards_n:
        x = 1
    c = 2 if replicas_n % 2 == 0 else 1
    return shards_n // x, x, replicas_n // c, c


class Net:
    def __init__(self, dims, send, recv):
        self.dims = dims
        _, nx, _, nc = dims
        s = lax.axis_index("shard")
        r = lax.axis_index("replica")
        self.at = [s // nx, s % nx, r // nc, r % nc]
        self.send, self.recv, self.used = send, recv, 0

    def device(self, axis, coordinate):
        place = list(self.at)
        place[axis] = coordinate
        return {
            "shard": place[0] * self.dims[1] + place[1],
            "replica": place[2] * self.dims[3] + place[3],
        }

    def peers(self, axis):
        n, me = self.dims[axis], self.at[axis]
        distances = sorted(range(1, n), key=lambda d: (min(d, n - d), d))
        return [((me + d) % n, (me + n - d) % n) for d in distances]

    def barrier(self):
        sem = pltpu.get_barrier_semaphore()
        count = 0
        for axis in range(4):
            for target, _ in self.peers(axis):
                pl.semaphore_signal(sem, inc=1, device_id=self.device(axis, target), device_id_type=MESH)
                count += 1
        pl.semaphore_wait(sem, count)

    def start(self, src, dst, axis, target):
        i = self.used
        self.used += 1
        copy = pltpu.make_async_remote_copy(
            src_ref=src,
            dst_ref=dst,
            send_sem=self.send.at[i],
            recv_sem=self.recv.at[i],
            device_id=self.device(axis, target),
            device_id_type=MESH,
        )
        copy.start()
        return copy


def gather_all(net, own, out, work=None):
    z, x, y, c = net.at
    piece = out.shape[-2]
    a, b = pl.ds(0, piece // 2), pl.ds(piece // 2, piece - piece // 2)
    sent = []

    def pair(view):
        for t, _ in net.peers(3):
            sent.append(net.start(view, view, 3, t))

    def spread(i, src):
        dst = out.at[i, x, y, c]
        along_x = [(net.start(src, dst, 1, t), f) for t, f in net.peers(1)]
        along_y = [(net.start(src, dst, 2, t), f) for t, f in net.peers(2)]
        for t, _ in net.peers(3):
            sent.append(net.start(src, dst, 3, t))
        return i, along_x, along_y

    def relay(i, along_x, along_y):
        corner = []
        for copy, f in along_x:
            copy.wait()
            view = out.at[i, f, y, c, a]
            corner += [(net.start(view, view, 2, t), out.at[i, f, g, c, a]) for t, g in net.peers(2)]
            pair(out.at[i, f, y, c])
        for copy, f in along_y:
            copy.wait()
            view = out.at[i, x, f, c, b]
            corner += [(net.start(view, view, 1, t), out.at[i, g, f, c, b]) for t, g in net.peers(1)]
            pair(out.at[i, x, f, c])
        return corner

    along_z = [(net.start(own, out.at[z, x, y, c], 0, t), f) for t, f in net.peers(0)]
    first = spread(z, own)
    if work is not None:
        work()
    corners = relay(*first)
    waves = []
    for copy, f in along_z:
        copy.wait()
        waves.append(spread(f, out.at[f, x, y, c]))
    for wave in waves:
        corners += relay(*wave)
    for copy, view in corners:
        copy.wait()
        pair(view)
    for copy in sent:
        copy.wait()


def copies_of(dims):
    nz, nx, ny, nc = dims
    x, y, c = nx - 1, ny - 1, nc - 1
    gathered = (nz - 1) + nz * (x + y + c + x * (y + c) + y * (x + c) + 2 * x * y * c)
    summed = nz * (c + 2 * x * y + x + y + 1)
    return 2 * gathered + summed + 4 * c + 5 * y + 2 * x + nz + 8


def prefetch(momentum, grad, m, g, local):
    loads = []
    size = m.shape[0] // CHUNKS
    for k in range(CHUNKS):
        rows = pl.ds(k * size, size)
        pair = [
            pltpu.make_async_copy(momentum.at[rows], m.at[rows], local.at[2 * k + 1]),
            pltpu.make_async_copy(grad.at[rows], g.at[rows], local.at[2 * k + 2]),
        ]
        for copy in pair:
            copy.start()
        loads.append((rows, pair))
    return loads


def sum_left(net, part, left, gram, rc, acc, ry, g, rgc, g1, rgy, g2, rgx, g3, gz):
    z, x, y, c = net.at
    copies = [net.start(part.at[:, t], rc.at[d], 3, t) for d, (t, _) in enumerate(net.peers(3))]
    for copy in copies:
        copy.wait()
    total = part[:, c]
    for d in range(len(copies)):
        total = total + rc[d]
    acc[...] = total
    copies = [net.start(acc.at[t], ry.at[d], 2, t) for d, (t, _) in enumerate(net.peers(2))]
    for copy in copies:
        copy.wait()
    own = acc[y]
    for d in range(len(copies)):
        own = own + ry[d]
    left[y, c] = own
    rows = [net.start(left.at[y, c], left.at[y, c], 2, t) for t, _ in net.peers(2)]
    product = lax.dot_general(own, own, (((0,), (0,)), ((), ())), precision=HIGHEST, preferred_element_type=F32)
    g[...] = product.reshape(g.shape)
    copies = [net.start(g.at[t], rgc.at[d], 3, t) for d, (t, _) in enumerate(net.peers(3))]
    for copy in copies:
        copy.wait()
    total = g[c]
    for d in range(len(copies)):
        total = total + rgc[d]
    g1[...] = total
    copies = [net.start(g1.at[t], rgy.at[d], 2, t) for d, (t, _) in enumerate(net.peers(2))]
    for copy in copies:
        copy.wait()
    total = g1[y]
    for d in range(len(copies)):
        total = total + rgy[d]
    g2[...] = total
    copies = [net.start(g2.at[t], rgx.at[d], 1, t) for d, (t, _) in enumerate(net.peers(1))]
    for copy in rows:
        copy.wait()
    rows = [net.start(left.at[:, c], left.at[:, c], 3, t) for t, _ in net.peers(3)]
    for copy in copies:
        copy.wait()
    total = g2[x]
    for d in range(len(copies)):
        total = total + rgx[d]
    g3[...] = total
    gz[z] = total
    copies = [net.start(g3, gz.at[z], 0, t) for t, _ in net.peers(0)]
    for copy in copies:
        copy.wait()
    total = gz[0]
    for d in range(1, gz.shape[0]):
        total = total + gz[d]
    gram[c, y, x] = total
    for axis, view in ((1, gram.at[c, y, x]), (2, gram.at[c, y]), (3, gram.at[c])):
        copies = [net.start(view, view, axis, t) for t, _ in net.peers(axis)]
        for copy in copies:
            copy.wait()
    for copy in rows:
        copy.wait()


def factor_inverse(block):
    n = block.shape[0]
    row = lax.broadcasted_iota(jnp.int32, (8, n), 0)
    lane = lax.broadcasted_iota(jnp.int32, (8, n), 1)
    parts = [
        jnp.concatenate([block[8 * i : 8 * i + 8, :], jnp.where(lane == row + 8 * i, 1.0, 0.0).astype(F32)], axis=1)
        for i in range(n // 8)
    ]
    ids = lax.broadcasted_iota(jnp.int32, (8, 2 * n), 0)
    for j in range(0, n, PIVOTS):
        first, o = j // 8, j % 8
        head = parts[first]
        s = {}
        for p in range(PIVOTS):
            for q in range(p, PIVOTS):
                s[p, q] = jnp.broadcast_to(head[o + p : o + p + 1, j + q : j + q + 1], (1, 2 * n))
        rows = [head[o + p : o + p + 1, :] for p in range(PIVOTS)]
        cols = [
            [jnp.broadcast_to(part[:, j + p : j + p + 1], (8, 2 * n)) for part in parts[first:]]
            for p in range(PIVOTS)
        ]
        total = None
        done = []
        for p in range(PIVOTS):
            r = lax.rsqrt(s[p, p])
            inv = r * r
            for q in range(p + 1, PIVOTS):
                t = s[p, q] * inv
                rows[q] = rows[q] - t * rows[p]
                cols[q] = [cq - t * cp for cq, cp in zip(cols[q], cols[p])]
                for w in range(q, PIVOTS):
                    s[q, w] = s[q, w] - t * s[p, w]
            done.append(rows[p] * r)
            scaled = rows[p] * inv
            terms = [cp * scaled for cp in cols[p]]
            total = terms if total is None else [u + v for u, v in zip(total, terms)]
        head = jnp.where(ids >= o + PIVOTS, head - total[0], head)
        for p in range(PIVOTS):
            head = jnp.where(ids == o + p, done[p], head)
        rest = [part - u for part, u in zip(parts[first + 1 :], total[1:])]
        parts = parts[:first] + [head] + rest
    return jnp.concatenate(parts, axis=0)[:, n:]


def orthonormal(gram, left, ortho, rounded, work, inverse):
    n = gram.shape[-1]
    row = lax.broadcasted_iota(jnp.int32, (n, n), 0)
    col = lax.broadcasted_iota(jnp.int32, (n, n), 1)
    work[:, :n] = gram[...].reshape(n, n)
    work[:, n:] = jnp.where(row == col, 1.0, 0.0).astype(F32)
    inverse[...] = jnp.zeros((n, n), F32)
    for lo in range(0, n, BLOCK):
        hi = lo + BLOCK
        start, end = hi // 128 * 128, (n + hi + 127) // 128 * 128
        corner = factor_inverse(work[lo:hi, lo:hi])
        upper = jnp.dot(corner, work[lo:hi, start:end], precision=HIGHEST, preferred_element_type=F32)
        inverse[lo:hi, : end - n] = upper[:, n - start :]
        if hi < n:
            work[hi:, start:end] -= lax.dot_general(
                upper[:, hi - start : n - start], upper, (((0,), (0,)), ((), ())),
                precision=HIGHEST, preferred_element_type=F32,
            )
    result = lax.dot_general(
        left[...].reshape(ortho.shape), inverse[...], (((1,), (1,)), ((), ())), precision=HIGHEST, preferred_element_type=F32
    )
    ortho[...] = result
    rounded[...] = result.astype(BF16)


def sum_right(net, buffer, ortho, out, part, sc, rc, acc, sa, ra, sb, rb, sx, rx, sy, ry, sz, rz, own):
    nz, nx, ny, nc = net.dims
    z, x, y, c = net.at
    xs, ys, cs = net.peers(1), net.peers(2), net.peers(3)
    targets = [t for t, _ in reversed(net.peers(0))] + [z]
    half = acc.shape[-2] // 2
    wide = buffer.shape[1] // nz
    corners = [(i, j) for j in range(ny - 1) for i in range(nx - 1)]
    pending = {}

    def multiply(k):
        columns = pl.ds(pl.multiple_of(targets[k] * wide, 128), wide)
        product = lax.dot_general(
            buffer[:, columns], ortho[...], (((0,), (0,)), ((), ())), preferred_element_type=F32
        )
        part[k] = product.reshape(part.shape[1:])
        copies = []
        for d, (t, _) in enumerate(cs):
            sc[d, k] = part[k, :, :, t].astype(BF16)
            copies.append(net.start(sc.at[d, k], rc.at[d, k], 3, t))
        pending[k] = copies

    def corner(k):
        for copy in pending[k]:
            copy.wait()
        total = part[k, :, :, c]
        for d in range(nc - 1):
            total = total + rc[d, k].astype(F32)
        acc[k] = total
        copies = []
        for e, (i, j) in enumerate(corners):
            tx, ty = xs[i][0], ys[j][0]
            sa[e, k] = acc[k, tx, ty, :half].astype(BF16)
            copies.append(net.start(sa.at[e, k], ra.at[e, k], 2, ty))
            sb[e, k] = acc[k, tx, ty, half:].astype(BF16)
            copies.append(net.start(sb.at[e, k], rb.at[e, k], 1, tx))
        pending[k] = copies

    def across(k):
        for copy in pending[k]:
            copy.wait()
        copies = []
        for i, (tx, _) in enumerate(xs):
            low = acc[k, tx, y, :half]
            for e, (p, _) in enumerate(corners):
                if p == i:
                    low = low + ra[e, k].astype(F32)
            sx[i, k, :half] = low.astype(BF16)
            sx[i, k, half:] = acc[k, tx, y, half:].astype(BF16)
            copies.append(net.start(sx.at[i, k], rx.at[i, k], 1, tx))
        for j, (ty, _) in enumerate(ys):
            high = acc[k, x, ty, half:]
            for e, (_, q) in enumerate(corners):
                if q == j:
                    high = high + rb[e, k].astype(F32)
            sy[j, k, :half] = acc[k, x, ty, :half].astype(BF16)
            sy[j, k, half:] = high.astype(BF16)
            copies.append(net.start(sy.at[j, k], ry.at[j, k], 2, ty))
        pending[k] = copies

    def along(k):
        for copy in pending[k]:
            copy.wait()
        total = acc[k, x, y]
        for i in range(nx - 1):
            total = total + rx[i, k].astype(F32)
        for j in range(ny - 1):
            total = total + ry[j, k].astype(F32)
        if k == nz - 1:
            return total
        sz[k] = total.astype(BF16)
        pending[k] = [net.start(sz.at[k], rz.at[k], 0, targets[k])]
        return None

    total = None
    for step in range(nz + 3):
        for lag, phase in ((3, along), (2, across), (1, corner), (0, multiply)):
            if 0 <= step - lag < nz:
                total = phase(step - lag)
                if lag == 3:
                    final = total
    for k in range(nz - 1):
        for copy in pending[k]:
            copy.wait()
        final = final + rz[k].astype(F32)
    mine = (final * (1.0 / (ny * nc))).astype(BF16)
    own[...] = mine
    out[z, x, y, c] = mine
    gather_all(net, own, out)


def kernel(dims, block, momentum, grad, right, ortho, rounded, prev, buffer, m, g, part, left, gram, *rest):
    lefts, (work, inverse), rights = rest[:11], rest[11:13], rest[13:-3]
    send, recv, local = rest[-3:]
    net = Net(dims, send, recv)
    z, x, y, c = net.at
    own = pltpu.make_async_copy(block.at[y, c], prev.at[z, x, y, c], local.at[0])
    own.start()
    loads = prefetch(momentum, grad, m, g, local)
    net.barrier()
    own.wait()

    def add():
        for rows, pair in loads:
            for copy in pair:
                copy.wait()
            buffer[rows, :] = (m[rows, :].astype(F32) + g[rows, :].astype(F32)).astype(BF16)

    gather_all(net, block.at[y, c], prev, add)
    width = buffer.shape[1]
    product = jnp.dot(buffer[...], prev[...].reshape(width, prev.shape[-1]), preferred_element_type=F32)
    part[...] = product.reshape(part.shape)
    sum_left(net, part, left, gram, *lefts)
    orthonormal(gram, left, ortho, rounded, work, inverse)
    sum_right(net, buffer, rounded, right, *rights)


def factors(dims, block, momentum, grad):
    nz, nx, ny, nc = dims
    rows, rank = block.shape
    width = momentum.shape[1]
    lp = rows // (ny * nc)
    rp = width // (nz * nx * ny * nc)
    gr = rank // (nc * ny * nx)
    pc, py, px, pz = max(nc - 1, 1), max(ny - 1, 1), max(nx - 1, 1), max(nz - 1, 1)
    pe, half = px * py, rp // 2
    full = (nz, nx, ny, nc, rp, rank)
    scratch = [
        ((nz, nx, ny, nc, lp, rank), BF16), (momentum.shape, BF16), (momentum.shape, BF16), (momentum.shape, BF16),
        ((ny, nc, lp, rank), F32), ((ny, nc, lp, rank), F32), ((nc, ny, nx, gr, rank), F32),
        ((pc, ny, lp, rank), F32), ((ny, lp, rank), F32), ((py, lp, rank), F32),
        ((nc, ny, nx, gr, rank), F32), ((pc, ny, nx, gr, rank), F32), ((ny, nx, gr, rank), F32),
        ((py, nx, gr, rank), F32), ((nx, gr, rank), F32), ((px, gr, rank), F32), ((gr, rank), F32),
        ((nz, gr, rank), F32),
        ((rank, 2 * rank), F32), ((rank, rank), F32),
        (full, F32),
        ((pc, nz, nx, ny, rp, rank), BF16), ((pc, nz, nx, ny, rp, rank), BF16),
        ((nz, nx, ny, rp, rank), F32),
        ((pe, nz, half, rank), BF16), ((pe, nz, half, rank), BF16),
        ((pe, nz, rp - half, rank), BF16), ((pe, nz, rp - half, rank), BF16),
        ((px, nz, rp, rank), BF16), ((px, nz, rp, rank), BF16),
        ((py, nz, rp, rank), BF16), ((py, nz, rp, rank), BF16),
        ((pz, rp, rank), BF16), ((pz, rp, rank), BF16),
        ((rp, rank), BF16),
    ]
    copies = copies_of(dims)
    vmem = pl.BlockSpec(memory_space=pltpu.VMEM)
    hbm = pl.BlockSpec(memory_space=pltpu.MemorySpace.HBM)
    right, ortho, rounded = pl.pallas_call(
        functools.partial(kernel, dims),
        out_shape=(
            jax.ShapeDtypeStruct(full, BF16),
            jax.ShapeDtypeStruct((rows, rank), F32),
            jax.ShapeDtypeStruct((rows, rank), BF16),
        ),
        in_specs=[vmem, hbm, hbm],
        out_specs=(vmem, vmem, vmem),
        scratch_shapes=[pltpu.VMEM(shape, kind) for shape, kind in scratch]
        + [pltpu.SemaphoreType.DMA((copies,))] * 2
        + [pltpu.SemaphoreType.DMA((2 * CHUNKS + 1,))],
        compiler_params=pltpu.CompilerParams(
            collective_id=0, has_side_effects=True, vmem_limit_bytes=50 << 20
        ),
    )(block.reshape(ny, nc, lp, rank), momentum, grad)
    return right.reshape(width, rank), ortho, rounded


def shards(dims, momentum, grad, right_prev):
    rows = grad.shape[2]
    width = grad.shape[3]
    rank = right_prev.shape[2]
    factor = width / math.sqrt(rank)
    buffer = momentum[0, 0].astype(F32) + grad[0, 0].astype(F32)
    right_full, ortho, ortho_b = factors(dims, right_prev[0], momentum[0, 0], grad[0, 0])
    wide = right_full.astype(F32)
    norms = jnp.sqrt(jnp.sum(wide * wide, axis=0) + epsilon_norm)
    right_own = lax.dynamic_slice_in_dim(right_full, lax.axis_index("shard") * rows, rows, axis=0)
    scaled = (ortho * (factor / norms)).astype(BF16)
    feedback = lax.dot_general(ortho_b, right_full, (((1,), (1,)), ((), ())), preferred_element_type=F32)
    momentum_new = (buffer - (1.0 - momentum_decay) * feedback).astype(BF16)
    stepped = lax.dot_general(scaled, right_full, (((1,), (1,)), ((), ())), preferred_element_type=F32)
    return momentum_new[None, None], stepped.astype(BF16)[None], right_own[None]


def solution(mesh):
    dims = grid_of(mesh.shape["shard"], mesh.shape["replica"])
    return jax.shard_map(
        functools.partial(shards, dims),
        mesh=mesh,
        in_specs=(
            P(None, "replica", "shard", None),
            P(None, "replica", "shard", None),
            P(None, "shard", None),
        ),
        out_specs=(
            P(None, "replica", "shard", None),
            P(None, "shard", None),
            P(None, "shard", None),
        ),
        check_vma=False,
    )
```

time: 133 us -> 109 us (0.82)
  Pallas kernels: 118 us -> 98.3 us
  matrix products: 10.7 us -> 7.28 us
    pallas_call x4 -> x1, Pallas kernels: 118 us -> 98.3 us  [factors(): pl.pallas_call(functools.partial(kernel, dims), out_shape=(jax.ShapeDtype...]
    dot_general x1 -> x0, matrix products: 3.44 us -> none  [shards(): local_left = jnp.dot(buffer_b, prev_full, preferred_element_type=F32)]
where the time goes in v3:
time: 109 us
  Pallas kernels  98.3 us (90%)
  matrix products  7.28 us (7%)
  local copies, waits for them, and re-layouts  1.68 us (2%)
    pallas_call x1, Pallas kernels, factors(): pl.pallas_call(functools.partial(kernel, dims), out_shape=(jax.ShapeDtype...  98.3 us
    dot_general x1, matrix products, shards(): lax.dot_general(ortho_b, right_full, (((1,), (1,)), ((), ())), preferred_...  3.96 us
    dot_general x1, matrix products, shards(): lax.dot_general(scaled, right_full, (((1,), (1,)), ((), ())), preferred_e...  3.31 us

profile of v3, /device:TPU:0, one launch (start us, length us, event | category | flops | bytes accessed | tf_op | source)
XLA Modules:
  0.0 108.5 jit_solution(17488387725558504353)
XLA Ops:
  0.6 0.0 copy-start
  0.6 0.9 copy-done
  1.6 98.3 %shard_map.58 = (bf16[4,2,2,2,128,256]{5,4,3,2,1,0:T(8,128)(2,1)S(1)}, f32[512,256]{1,0:T(8,128)S(1)}, bf16[512,256]{1,0:T(8,128)(2,1)S(1)}) custom-call(bf16[2,2,128,256]{3,2,1,0:T(8,128)(2,1)S(1)} %bitcast.18, bf16[512,4096]{1,0:T(8,128)(2,1)} %bitcast.19, bf16[512,4096]{1,0:T(8,128)(2,1)} %bitcast.20), custom_call_target="tpu_custom_call" | custom-call | tf_op jit(solution)/shard_map/pallas_call | solution.py:425
  99.9 0.0 copy-start.2
  99.9 0.6 multiply_reduce_fusion
  100.5 0.0 copy-start.1
  100.5 0.7 dynamic-slice_bitcast_fusion
  101.2 3.3 %fusion = bf16[1,512,4096]{2,1,0:T(8,128)(2,1)} fusion(bf16[4096,256]{1,0:T(8,128)(2,1)S(1)} %bitcast.16, f32[512,256]{1,0:T(8,128)S(1)} %get-tuple-element.8, f32[256]{0:T(256)S(1)} %rsqrt_multiply_fusion), kind=kOutput, calls=%fused_computation.2 | convolution fusion | flops 1076101120 | bytes 6816768 | tf_op jit(solution)/shard_map/dot_general | solution.py:457
  104.5 0.0 copy-done.2
  104.5 0.0 copy-done.1
  104.5 4.0 %fusion.1 = bf16[1,1,512,4096]{3,2,1,0:T(8,128)(2,1)} fusion(bf16[512,256]{1,0:T(8,128)(2,1)S(1)} %get-tuple-element.6, bf16[4096,256]{1,0:T(8,128)(2,1)S(1)} %bitcast.17, bf16[1,1,512,4096]{3,2,1,0:T(8,128)(2,1)S(1)} %copy-done.2, bf16[1,1,512,4096]{3,2,1,0:T(8,128)(2,1)S(1)} %copy-done.1), kind=kOutput, calls=%fused_computation.3 | convolution fusion | flops 1086324736 | bytes 14942208 | tf_op jit(solution)/shard_map/dot_general | solution.py:455
  (1 shorter events, 0.0 us)
Async XLA Ops:
  0.6 1.0 copy-start
  99.9 4.7 %copy-start.2 = (bf16[1,1,512,4096]{3,2,1,0:T(8,128)(2,1)S(1)}, bf16[1,1,512,4096]{3,2,1,0:T(8,128)(2,1)}, u32[]{:S(2)}) copy-start(bf16[1,1,512,4096]{3,2,1,0:T(8,128)(2,1)} %param.4) | copy-start | bytes 12582916
  100.5 4.1 %copy-start.1 = (bf16[1,1,512,4096]{3,2,1,0:T(8,128)(2,1)S(1)}, bf16[1,1,512,4096]{3,2,1,0:T(8,128)(2,1)}, u32[]{:S(2)}) copy-start(bf16[1,1,512,4096]{3,2,1,0:T(8,128)(2,1)} %param.3) | copy-start | bytes 12582916

commit v4 on v3

--- a/solution.py
+++ b/solution.py
@@ -17,6 +17,7 @@
 BLOCK = 64
 PIVOTS = 4
 CHUNKS = 8
+TILES = 8
 
 
 def grid_of(shards_n, replicas_n):
@@ -38,7 +39,10 @@
 
     def device(self, axis, coordinate):
         place = list(self.at)
-        place[axis] = coordinate
+        if axis is None:
+            place[1], place[2] = coordinate
+        else:
+            place[axis] = coordinate
         return {
             "shard": place[0] * self.dims[1] + place[1],
             "replica": place[2] * self.dims[3] + place[3],
@@ -48,6 +52,14 @@
         n, me = self.dims[axis], self.at[axis]
         distances = sorted(range(1, n), key=lambda d: (min(d, n - d), d))
         return [((me + d) % n, (me + n - d) % n) for d in distances]
+
+    def plane(self):
+        nx, ny = self.dims[1:3]
+        x, y = self.at[1:3]
+        steps = sorted(((i, j) for i in range(nx) for j in range(ny) if i or j), key=lambda p: (min(p[0], nx - p[0]) + min(p[1], ny - p[1]), p))
+        return [
+            (((x + i) % nx, (y + j) % ny), ((x + nx - i) % nx, (y + ny - j) % ny)) for i, j in steps
+        ]
 
     def barrier(self):
         sem = pltpu.get_barrier_semaphore()
@@ -56,6 +68,9 @@
             for target, _ in self.peers(axis):
                 pl.semaphore_signal(sem, inc=1, device_id=self.device(axis, target), device_id_type=MESH)
                 count += 1
+        for target, _ in self.plane():
+            pl.semaphore_signal(sem, inc=1, device_id=self.device(None, target), device_id_type=MESH)
+            count += 1
         pl.semaphore_wait(sem, count)
 
     def start(self, src, dst, axis, target):
@@ -73,13 +88,12 @@
         return copy
 
 
-def gather_all(net, own, out, work=None):
+def gather_all(net, own, out, work=None, use=None):
     z, x, y, c = net.at
     piece = out.shape[-2]
     a, b = pl.ds(0, piece // 2), pl.ds(piece // 2, piece - piece // 2)
-    sent = []
-
-    def pair(view):
+
+    def pair(view, sent):
         for t, _ in net.peers(3):
             sent.append(net.start(view, view, 3, t))
 
@@ -87,40 +101,42 @@
         dst = out.at[i, x, y, c]
         along_x = [(net.start(src, dst, 1, t), f) for t, f in net.peers(1)]
         along_y = [(net.start(src, dst, 2, t), f) for t, f in net.peers(2)]
-        for t, _ in net.peers(3):
-            sent.append(net.start(src, dst, 3, t))
-        return i, along_x, along_y
-
-    def relay(i, along_x, along_y):
+        sent = [net.start(src, dst, 3, t) for t, _ in net.peers(3)]
+        return i, along_x, along_y, sent
+
+    def relay(i, along_x, along_y, sent):
         corner = []
         for copy, f in along_x:
             copy.wait()
             view = out.at[i, f, y, c, a]
             corner += [(net.start(view, view, 2, t), out.at[i, f, g, c, a]) for t, g in net.peers(2)]
-            pair(out.at[i, f, y, c])
+            pair(out.at[i, f, y, c], sent)
         for copy, f in along_y:
             copy.wait()
             view = out.at[i, x, f, c, b]
             corner += [(net.start(view, view, 1, t), out.at[i, g, f, c, b]) for t, g in net.peers(1)]
-            pair(out.at[i, x, f, c])
-        return corner
+            pair(out.at[i, x, f, c], sent)
+        return i, corner, sent
 
     along_z = [(net.start(own, out.at[z, x, y, c], 0, t), f) for t, f in net.peers(0)]
     first = spread(z, own)
     if work is not None:
         work()
-    corners = relay(*first)
+    relayed = [relay(*first)]
     waves = []
     for copy, f in along_z:
         copy.wait()
         waves.append(spread(f, out.at[f, x, y, c]))
-    for wave in waves:
-        corners += relay(*wave)
-    for copy, view in corners:
-        copy.wait()
-        pair(view)
-    for copy in sent:
-        copy.wait()
+    relayed += [relay(*wave) for wave in waves]
+    for i, corner, sent in relayed:
+        for copy, view in corner:
+            copy.wait()
+            pair(view, sent)
+    for i, corner, sent in relayed:
+        for copy in sent:
+            copy.wait()
+        if use is not None:
+            use(i)
 
 
 def copies_of(dims):
@@ -128,7 +144,7 @@
     x, y, c = nx - 1, ny - 1, nc - 1
     gathered = (nz - 1) + nz * (x + y + c + x * (y + c) + y * (x + c) + 2 * x * y * c)
     summed = nz * (c + 2 * x * y + x + y + 1)
-    return 2 * gathered + summed + 4 * c + 5 * y + 2 * x + nz + 8
+    return 2 * gathered + summed + 4 * c + 3 * y + 2 * nx * ny + nz + 8
 
 
 def prefetch(momentum, grad, m, g, local):
@@ -146,7 +162,7 @@
     return loads
 
 
-def sum_left(net, part, left, gram, rc, acc, ry, g, rgc, g1, rgy, g2, rgx, g3, gz):
+def sum_left(net, part, left, gram, rc, acc, ry, g, rgc, g1, rg, g3, gz):
     z, x, y, c = net.at
     copies = [net.start(part.at[:, t], rc.at[d], 3, t) for d, (t, _) in enumerate(net.peers(3))]
     for copy in copies:
@@ -172,22 +188,15 @@
     for d in range(len(copies)):
         total = total + rgc[d]
     g1[...] = total
-    copies = [net.start(g1.at[t], rgy.at[d], 2, t) for d, (t, _) in enumerate(net.peers(2))]
-    for copy in copies:
-        copy.wait()
-    total = g1[y]
-    for d in range(len(copies)):
-        total = total + rgy[d]
-    g2[...] = total
-    copies = [net.start(g2.at[t], rgx.at[d], 1, t) for d, (t, _) in enumerate(net.peers(1))]
+    copies = [net.start(g1.at[t[1], t[0]], rg.at[e], None, t) for e, (t, _) in enumerate(net.plane())]
     for copy in rows:
         copy.wait()
     rows = [net.start(left.at[:, c], left.at[:, c], 3, t) for t, _ in net.peers(3)]
     for copy in copies:
         copy.wait()
-    total = g2[x]
-    for d in range(len(copies)):
-        total = total + rgx[d]
+    total = g1[y, x]
+    for e in range(len(copies)):
+        total = total + rg[e]
     g3[...] = total
     gz[z] = total
     copies = [net.start(g3, gz.at[z], 0, t) for t, _ in net.peers(0)]
@@ -197,11 +206,12 @@
     for d in range(1, gz.shape[0]):
         total = total + gz[d]
     gram[c, y, x] = total
-    for axis, view in ((1, gram.at[c, y, x]), (2, gram.at[c, y]), (3, gram.at[c])):
-        copies = [net.start(view, view, axis, t) for t, _ in net.peers(axis)]
-        for copy in copies:
-            copy.wait()
-    for copy in rows:
+    view = gram.at[c, y, x]
+    copies = [net.start(view, view, None, t) for t, _ in net.plane()]
+    for copy in copies:
+        copy.wait()
+    copies = [net.start(gram.at[c], gram.at[c], 3, t) for t, _ in net.peers(3)]
+    for copy in copies + rows:
         copy.wait()
 
 
@@ -274,7 +284,7 @@
     rounded[...] = result.astype(BF16)
 
 
-def sum_right(net, buffer, ortho, out, part, sc, rc, acc, sa, ra, sb, rb, sx, rx, sy, ry, sz, rz, own):
+def sum_right(net, use, buffer, ortho, out, part, sc, rc, acc, sa, ra, sb, rb, sx, rx, sy, ry, sz, rz, own):
     nz, nx, ny, nc = net.dims
     z, x, y, c = net.at
     xs, ys, cs = net.peers(1), net.peers(2), net.peers(3)
@@ -362,11 +372,11 @@
     mine = (final * (1.0 / (ny * nc))).astype(BF16)
     own[...] = mine
     out[z, x, y, c] = mine
-    gather_all(net, own, out)
-
-
-def kernel(dims, block, momentum, grad, right, ortho, rounded, prev, buffer, m, g, part, left, gram, *rest):
-    lefts, (work, inverse), rights = rest[:11], rest[11:13], rest[13:-3]
+    gather_all(net, own, out, use=use)
+
+
+def kernel(dims, block, momentum, grad, right, ortho, rounded, moved, squares, prev, buffer, m, g, part, left, gram, *rest):
+    lefts, (work, inverse), rights = rest[:9], rest[9:11], rest[11:-3]
     send, recv, local = rest[-3:]
     net = Net(dims, send, recv)
     z, x, y, c = net.at
@@ -388,7 +398,69 @@
     part[...] = product.reshape(part.shape)
     sum_left(net, part, left, gram, *lefts)
     orthonormal(gram, left, ortho, rounded, work, inverse)
-    sum_right(net, buffer, rounded, right, *rights)
+    squares[...] = jnp.zeros(squares.shape, F32)
+    wide = width // dims[0]
+    size = min(wide, 512)
+
+    def use(i):
+        rows = right[i].reshape(wide, right.shape[-1])
+        square = rows.astype(F32)
+        squares[0:1] = squares[0:1] + jnp.sum(square * square, axis=0, keepdims=True)
+        for k in range(0, wide, size):
+            columns = pl.ds(pl.multiple_of(i * wide + k, 128), size)
+            feedback = lax.dot_general(
+                rounded[...], rows[k : k + size], (((1,), (1,)), ((), ())), preferred_element_type=F32
+            )
+            total = m[:, columns].astype(F32) + g[:, columns].astype(F32)
+            moved[:, columns] = (total - (1.0 - momentum_decay) * feedback).astype(BF16)
+
+    sum_right(net, use, buffer, rounded, right, *rights)
+
+
+def finish_kernel(factor, right, ortho, moved, squares, momentum_new, update, own, stage, sem):
+    rows, rank = ortho.shape
+    width = right.shape[0]
+    first = pltpu.make_async_copy(moved, momentum_new, sem.at[0])
+    first.start()
+    start = pl.multiple_of(lax.axis_index("shard") * rows, rows)
+    second = pltpu.make_async_copy(right.at[pl.ds(start, rows)], own, sem.at[1])
+    second.start()
+    norms = jnp.sqrt(squares[0:1, :] + epsilon_norm)
+    scaled = (ortho[...] * (factor / norms)).astype(BF16)
+    size = width // TILES
+    copies = [first, second]
+    for k in range(TILES):
+        columns = slice(k * size, (k + 1) * size)
+        stage[k] = lax.dot_general(
+            scaled, right[columns, :], (((1,), (1,)), ((), ())), preferred_element_type=F32
+        ).astype(BF16)
+        copy = pltpu.make_async_copy(stage.at[k], update.at[:, columns], sem.at[2 + k])
+        copy.start()
+        copies.append(copy)
+    for copy in copies:
+        copy.wait()
+
+
+def finish(right, ortho, moved, squares):
+    width, rank = right.shape
+    rows = ortho.shape[0]
+    vmem = pl.BlockSpec(memory_space=pltpu.VMEM)
+    hbm = pl.BlockSpec(memory_space=pltpu.MemorySpace.HBM)
+    return pl.pallas_call(
+        functools.partial(finish_kernel, width / math.sqrt(rank)),
+        out_shape=(
+            jax.ShapeDtypeStruct(moved.shape, BF16),
+            jax.ShapeDtypeStruct(moved.shape, BF16),
+            jax.ShapeDtypeStruct((rows, rank), BF16),
+        ),
+        in_specs=[vmem] * 4,
+        out_specs=(hbm, hbm, hbm),
+        scratch_shapes=[
+            pltpu.VMEM((TILES, rows, width // TILES), BF16),
+            pltpu.SemaphoreType.DMA((2 + TILES,)),
+        ],
+        compiler_params=pltpu.CompilerParams(vmem_limit_bytes=12 << 20),
+    )(right, ortho, moved, squares)
 
 
 def factors(dims, block, momentum, grad):
@@ -406,7 +478,7 @@
         ((ny, nc, lp, rank), F32), ((ny, nc, lp, rank), F32), ((nc, ny, nx, gr, rank), F32),
         ((pc, ny, lp, rank), F32), ((ny, lp, rank), F32), ((py, lp, rank), F32),
         ((nc, ny, nx, gr, rank), F32), ((pc, ny, nx, gr, rank), F32), ((ny, nx, gr, rank), F32),
-        ((py, nx, gr, rank), F32), ((nx, gr, rank), F32), ((px, gr, rank), F32), ((gr, rank), F32),
+        ((max(nx * ny - 1, 1), gr, rank), F32), ((gr, rank), F32),
         ((nz, gr, rank), F32),
         ((rank, 2 * rank), F32), ((rank, rank), F32),
         (full, F32),
@@ -422,40 +494,31 @@
     copies = copies_of(dims)
     vmem = pl.BlockSpec(memory_space=pltpu.VMEM)
     hbm = pl.BlockSpec(memory_space=pltpu.MemorySpace.HBM)
-    right, ortho, rounded = pl.pallas_call(
+    right, ortho, _, moved, squares = pl.pallas_call(
         functools.partial(kernel, dims),
         out_shape=(
             jax.ShapeDtypeStruct(full, BF16),
             jax.ShapeDtypeStruct((rows, rank), F32),
             jax.ShapeDtypeStruct((rows, rank), BF16),
+            jax.ShapeDtypeStruct(momentum.shape, BF16),
+            jax.ShapeDtypeStruct((8, rank), F32),
         ),
         in_specs=[vmem, hbm, hbm],
-        out_specs=(vmem, vmem, vmem),
+        out_specs=(vmem,) * 5,
         scratch_shapes=[pltpu.VMEM(shape, kind) for shape, kind in scratch]
         + [pltpu.SemaphoreType.DMA((copies,))] * 2
         + [pltpu.SemaphoreType.DMA((2 * CHUNKS + 1,))],
         compiler_params=pltpu.CompilerParams(
-            collective_id=0, has_side_effects=True, vmem_limit_bytes=50 << 20
+            collective_id=0, has_side_effects=True, vmem_limit_bytes=36 << 20
         ),
     )(block.reshape(ny, nc, lp, rank), momentum, grad)
-    return right.reshape(width, rank), ortho, rounded
+    return right.reshape(width, rank), ortho, moved, squares
 
 
 def shards(dims, momentum, grad, right_prev):
-    rows = grad.shape[2]
-    width = grad.shape[3]
-    rank = right_prev.shape[2]
-    factor = width / math.sqrt(rank)
-    buffer = momentum[0, 0].astype(F32) + grad[0, 0].astype(F32)
-    right_full, ortho, ortho_b = factors(dims, right_prev[0], momentum[0, 0], grad[0, 0])
-    wide = right_full.astype(F32)
-    norms = jnp.sqrt(jnp.sum(wide * wide, axis=0) + epsilon_norm)
-    right_own = lax.dynamic_slice_in_dim(right_full, lax.axis_index("shard") * rows, rows, axis=0)
-    scaled = (ortho * (factor / norms)).astype(BF16)
-    feedback = lax.dot_general(ortho_b, right_full, (((1,), (1,)), ((), ())), preferred_element_type=F32)
-    momentum_new = (buffer - (1.0 - momentum_decay) * feedback).astype(BF16)
-    stepped = lax.dot_general(scaled, right_full, (((1,), (1,)), ((), ())), preferred_element_type=F32)
-    return momentum_new[None, None], stepped.astype(BF16)[None], right_own[None]
+    right, ortho, moved, squares = factors(dims, right_prev[0], momentum[0, 0], grad[0, 0])
+    momentum_new, update, right_own = finish(right, ortho, moved, squares)
+    return momentum_new[None, None], update[None], right_own[None]
 
 
 def solution(mesh):

time: 109 us -> 105 us (0.963)
  matrix products: 7.28 us -> 0 us
  local copies, waits for them, and re-layouts: 1.68 us -> 5.32 us
    dot_general x2 -> x0, matrix products: 7.28 us -> none  [the longest x1 3.96 us: shards(): lax.dot_general(ortho_b, right_full, (((1,), (1,)), ((), ())), preferred_...]
    unnamed x6, local copies, waits for them, and re-layouts: 0.95 us -> 5.32 us
    pallas_call x0 -> x1, Pallas kernels: none -> 3.46 us  [finish(): pl.pallas_call(functools.partial(finish_kernel, width / math.sqrt(rank)),...]
    pallas_call x1, Pallas kernels: 98.3 us -> 94.9 us  [factors(): pl.pallas_call(functools.partial(kernel, dims), out_shape=(jax.ShapeDtype...]
where the time goes in v4:
time: 105 us; the launch traced here: 104 us
  Pallas kernels  98.3 us (94%)
  local copies, waits for them, and re-layouts  5.32 us (5%)
    pallas_call x1, Pallas kernels, factors(): pl.pallas_call(functools.partial(kernel, dims), out_shape=(jax.ShapeDtype...  94.9 us
    unnamed x6, local copies, waits for them, and re-layouts  5.32 us
    pallas_call x1, Pallas kernels, finish(): pl.pallas_call(functools.partial(finish_kernel, width / math.sqrt(rank)),...  3.46 us

profile of v4, /device:TPU:0, one launch (start us, length us, event | category | flops | bytes accessed | tf_op | source)
XLA Modules:
  0.0 104.5 jit_solution(2597152206219651472)
XLA Ops:
  0.6 0.0 copy-start
  0.6 2.2 %copy-done = bf16[1,1,512,4096]{3,2,1,0:T(8,128)(2,1)S(1)} copy-done((bf16[1,1,512,4096]{3,2,1,0:T(8,128)(2,1)S(1)}, bf16[1,1,512,4096]{3,2,1,0:T(8,128)(2,1)}, u32[]{:S(2)}) %copy-start) | copy-done | bytes 4194328
  2.8 0.0 copy-start.1
  2.8 2.2 %copy-done.1 = bf16[1,1,512,4096]{3,2,1,0:T(8,128)(2,1)S(1)} copy-done((bf16[1,1,512,4096]{3,2,1,0:T(8,128)(2,1)S(1)}, bf16[1,1,512,4096]{3,2,1,0:T(8,128)(2,1)}, u32[]{:S(2)}) %copy-start.1) | copy-done | bytes 4194328
  5.0 0.0 copy-start.2
  5.0 0.9 copy-done.2
  6.0 94.9 %shard_map.58 = (bf16[4,2,2,2,128,256]{5,4,3,2,1,0:T(8,128)(2,1)S(1)}, f32[512,256]{1,0:T(8,128)S(1)}, bf16[512,256]{1,0:T(8,128)(2,1)}, bf16[512,4096]{1,0:T(8,128)(2,1)S(1)}, f32[8,256]{1,0:T(8,128)S(1)}) custom-call(bf16[2,2,128,256]{3,2,1,0:T(8,128)(2,1)S(1)} %bitcast.10, bf16[512,4096]{1,0:T(8,128)(2,1)S(1)} %bitcast.7, bf16[512,4096]{1,0:T(8,128)(2,1)S(1)} %bitcast.8), custom_call_target="tpu_custom_call" | custom-call | tf_op jit(solution)/shard_map/pallas_call | solution.py:497
  100.8 3.5 %shard_map.59 = (bf16[512,4096]{1,0:T(8,128)(2,1)}, bf16[512,4096]{1,0:T(8,128)(2,1)}, bf16[512,256]{1,0:T(8,128)(2,1)}) custom-call(bf16[4096,256]{1,0:T(8,128)(2,1)S(1)} %bitcast.9, f32[512,256]{1,0:T(8,128)S(1)} %get-tuple-element.11.ortho, bf16[512,4096]{1,0:T(8,128)(2,1)S(1)} %get-tuple-element.12.moved, f32[8,256]{1,0:T(8,128)S(1)} %get-tuple-element.13.squares), custom_call_target="tpu_custom_call" | custom-call | tf_op jit(solution)/shard_map/pallas_call | solution.py:449
Async XLA Ops:
  0.6 2.2 %copy-start = (bf16[1,1,512,4096]{3,2,1,0:T(8,128)(2,1)S(1)}, bf16[1,1,512,4096]{3,2,1,0:T(8,128)(2,1)}, u32[]{:S(2)}) copy-start(bf16[1,1,512,4096]{3,2,1,0:T(8,128)(2,1)} %param.3) | copy-start | bytes 12582916
  2.8 2.2 %copy-start.1 = (bf16[1,1,512,4096]{3,2,1,0:T(8,128)(2,1)S(1)}, bf16[1,1,512,4096]{3,2,1,0:T(8,128)(2,1)}, u32[]{:S(2)}) copy-start(bf16[1,1,512,4096]{3,2,1,0:T(8,128)(2,1)} %param.4) | copy-start | bytes 12582916
  5.0 0.9 copy-start.2

commit v5 on v4

--- a/solution.py
+++ b/solution.py
@@ -511,7 +511,7 @@
         compiler_params=pltpu.CompilerParams(
             collective_id=0, has_side_effects=True, vmem_limit_bytes=36 << 20
         ),
-    )(block.reshape(ny, nc, lp, rank), momentum, grad)
+    )(block.reshape(ny, nc, lp, rank), pltpu.with_memory_space_constraint(momentum, pltpu.MemorySpace.HBM), pltpu.with_memory_space_constraint(grad, pltpu.MemorySpace.HBM))
     return right.reshape(width, rank), ortho, moved, squares
 
 

time: 105 us -> 99.7 us (0.950)
  local copies, waits for them, and re-layouts: 5.32 us -> 0.94 us
    unnamed x6 -> x2, local copies, waits for them, and re-layouts: 5.32 us -> 0.94 us
where the time goes in v5:
time: 99.7 us; the launch traced here: 99.5 us
  Pallas kernels  97.8 us (98%)
    pallas_call x1, Pallas kernels, factors(): pl.pallas_call(functools.partial(kernel, dims), out_shape=(jax.ShapeDtype...  94.3 us
    pallas_call x1, Pallas kernels, finish(): pl.pallas_call(functools.partial(finish_kernel, width / math.sqrt(rank)),...  3.46 us

profile of v5, /device:TPU:0, one launch (start us, length us, event | category | flops | bytes accessed | tf_op | source)
XLA Modules:
  0.0 99.5 jit_solution(7786283011948004518)
XLA Ops:
  0.6 0.0 copy-start
  0.6 0.9 copy-done
  1.6 94.3 %shard_map.58 = (bf16[4,2,2,2,128,256]{5,4,3,2,1,0:T(8,128)(2,1)S(1)}, f32[512,256]{1,0:T(8,128)S(1)}, bf16[512,256]{1,0:T(8,128)(2,1)}, bf16[512,4096]{1,0:T(8,128)(2,1)S(1)}, f32[8,256]{1,0:T(8,128)S(1)}) custom-call(bf16[2,2,128,256]{3,2,1,0:T(8,128)(2,1)S(1)} %bitcast.8, bf16[512,4096]{1,0:T(8,128)(2,1)} %bitcast.9, bf16[512,4096]{1,0:T(8,128)(2,1)} %bitcast.10), custom_call_target="tpu_custom_call" | custom-call | tf_op jit(solution)/shard_map/pallas_call | solution.py:497
  95.9 3.5 %shard_map.59 = (bf16[512,4096]{1,0:T(8,128)(2,1)}, bf16[512,4096]{1,0:T(8,128)(2,1)}, bf16[512,256]{1,0:T(8,128)(2,1)}) custom-call(bf16[4096,256]{1,0:T(8,128)(2,1)S(1)} %bitcast.7, f32[512,256]{1,0:T(8,128)S(1)} %get-tuple-element.11.ortho, bf16[512,4096]{1,0:T(8,128)(2,1)S(1)} %get-tuple-element.12.moved, f32[8,256]{1,0:T(8,128)S(1)} %get-tuple-element.13.squares), custom_call_target="tpu_custom_call" | custom-call | tf_op jit(solution)/shard_map/pallas_call | solution.py:449
Async XLA Ops:
  0.6 1.0 copy-start
